TPU v7x, 32 devices: a whole 2x2x4 slice. The times are simulated.
32 devices in a mesh: row: 8 (over y, x, core), col: 4 (over z).
Axes of the slice: x: 2, y: 2, z: 4, core: 2. Of those that a mesh axis runs over, the one named last changes fastest.
Arguments:
- database: bfloat16 [4096, 16384], P('row', 'col'), may hold values from -1 to 1
- query: bfloat16 [64, 4096], P('col', 'row'), may hold values from -8 to 8
- slot_map: int32 [64], replicated, may hold values from 0 to 63, each once
- keys: bfloat16 [64, 2048, 512], P(('row', 'col')), may hold values from -0.125 to 0.125
Outputs:
- packed: float32 [64, 8, 512], P(('row', 'col'))
Inputs may be any that keep to these rules, and one draw needn't show every extreme that they name: `slot_map`: each slot serves a different client.
All inputs are finite; a program needn't handle non-finite values.
Results may differ from a plain program's by a relative error of at most 0.0085.
Values may be sent and summed in bfloat16 or wider, within the bound.
No kernel may reach another device: no remote copies, remote signals or barrier semaphores. Data moves between devices by JAX's collectives and lax.ppermute only.
A program may use at most 64 MiB of HBM per device.

v0:
```python
import jax
import jax.numpy as jnp
from jax import lax
from jax.sharding import PartitionSpec as P


def shards(database, query, slot_map, keys):
    rows_axis = lax.axis_size("row")
    cols_axis = lax.axis_size("col")
    factor = float(database.shape[0] * rows_axis) ** (-0.5)
    gathered = lax.all_gather(query, "col", axis=0, tiled=True)
    total = gathered.shape[0]
    owned_count = total // (rows_axis * cols_axis)
    chosen = jnp.take(gathered, slot_map, axis=0)
    partial_value = jnp.dot(chosen, database, preferred_element_type=jnp.float32)
    block = lax.psum_scatter(partial_value, "row", scatter_dimension=0, tiled=True)
    owned = lax.all_to_all(
        block.astype(jnp.bfloat16), "col", split_axis=0, concat_axis=1, tiled=True
    ).astype(block.dtype)
    switched = (owned * factor).astype(jnp.bfloat16)
    tiles = switched.reshape(owned_count, -1, keys.shape[1])
    return jnp.einsum("ptj,pjk->ptk", tiles, keys, preferred_element_type=jnp.float32)


def solution(mesh):
    placed = (P("row", "col"), P("col", "row"), P(), P(("row", "col"), None, None))
    return jax.shard_map(
        shards, mesh=mesh, in_specs=placed, out_specs=P(("row", "col"), None, None), check_vma=False
    )
```

profile of v0, /device:TPU:0, one launch (start us, length us, event | category | flops | bytes accessed | tf_op | source)
XLA Modules:
  0.0 86.6 jit_solution(4288527621348501784)
XLA Ops:
  6.5 0.0 reduce-scatter.2.cloned.1.call-start
  6.5 0.7 compare_and_fusion
  7.2 0.7 compare_select_fusion
  7.9 15.1 %all_gather.3 = bf16[64,512]{1,0:T(8,128)(2,1)S(1)} all-gather(bf16[16,512]{1,0:T(8,128)(2,1)} %param.5), channel_id=1, replica_groups=mesh['row'=8,'col'=4] {'col'}, dimensions={0}, use_global_device_ids=true | all-gather | bytes 81920 | tf_op jit(solution)/shard_map/all_gather | solution.py:11
  23.0 0.7 gather_fusion
  23.7 4.1 %fusion.1 = f32[64,4096]{1,0:T(8,128)} fusion(bf16[512,4096]{1,0:T(8,128)(2,1)} %param.4, bf16[64,512]{1,0:T(8,128)(2,1)S(1)} %gather_fusion, pred[64]{0:T(512)(128)(4,1)S(1)} %compare_and_fusion), kind=kOutput, calls=%fused_computation.3 | convolution fusion | flops 268468224 | bytes 5308480 | tf_op jit(solution)/shard_map/dot_general | solution.py:15
  27.8 0.0 reduce-scatter.2.cloned.1.call-update
  27.8 37.3 %reduce-scatter.2.cloned.1.call-done = f32[8,4096]{1,0:T(8,128)} async-done(((f32[64,4096]{1,0:T(8,128)}), f32[8,4096]{1,0:T(8,128)}) %reduce-scatter.2.cloned.1.call-update) | async-done | bytes 131088 | tf_op jit(solution)/shard_map/reduce_scatter | solution.py:16
  65.1 0.9 %convert_element_type.19 = bf16[8,4096]{1,0:T(8,128)(2,1)S(1)} convert(f32[8,4096]{1,0:T(8,128)} %reduce-scatter.2.cloned.1.call-done) | non-fusion elementwise | flops 32768 | bytes 196608 | tf_op jit(solution)/shard_map/convert_element_type | solution.py:18
  66.0 0.1 all_to_all.10
  66.0 10.1 %all_to_all.13 = bf16[4,2,4096]{2,1,0:T(2,128)(2,1)S(1)} all-to-all(bf16[4,2,4096]{2,1,0:T(2,128)(2,1)S(1)} %all_to_all.10), channel_id=1, replica_groups=mesh['row'=8,'col'=4] {'col'}, dimensions={0} | all-to-all | bytes 131072 | tf_op jit(solution)/shard_map/all_to_all | solution.py:17
  76.2 0.1 fusion
  76.2 0.1 copy.5
  76.3 3.5 %fusion.6 = f32[2,8,512]{2,1,0:T(8,128)} fusion(bf16[2,8,2048]{2,1,0:T(8,128)(2,1)S(1)} %convert_element_type.23, bf16[2,2048,512]{2,1,0:T(8,128)(2,1)} %param.7), kind=kOutput, calls=%fused_computation.11 | convolution fusion | flops 33554432 | bytes 4292608 | tf_op jit(solution)/shard_map/ptj,pjk->ptk/dot_general | solution.py:22
  (2 shorter events, 0.0 us)
Async XLA Ops:
  6.5 58.5 %reduce-scatter.2.cloned.1.call-start = ((), (), s32[]{:S(2)}) async-start(), calls=%async_computation.2 | async-start | bytes 1179648 | tf_op jit(solution)/shard_map/reduce_scatter | solution.py:16
Sparse Core Ops, SparseCore 0:
  27.9 37.1 reduce-scatter.1
where the time goes:
time: 86.9 us; the launch traced here: 86.6 us
  waiting for transfers between devices  37.3 us (43%)
  blocking collectives  25.3 us (29%)
  between operations  13.4 us (15%)
  matrix products  7.53 us (9%)
  other arithmetic  2.3 us (3%)
    reduce_scatter x1, waiting for transfers between devices, shards(): lax.psum_scatter(partial_value, 'row', scatter_dimension=0, tiled=True)  37.3 us
    all_gather x1, blocking collectives, shards(): gathered = lax.all_gather(query, 'col', axis=0, tiled=True)  15.1 us
    all_to_all x1, blocking collectives, shards(): lax.all_to_all(block.astype(jnp.bfloat16), 'col', split_axis=0, concat_ax...  10.1 us
    dot_general x1, matrix products, shards(): jnp.dot(chosen, database, preferred_element_type=jnp.float32)  4.07 us
    dot_general x1, matrix products, shards(): jnp.einsum('ptj,pjk->ptk', tiles, keys, preferred_element_type=jnp.float32)  3.46 us
  transfers between devices with their start and end apart: 1, of which 1 were waited for; matrix products, arithmetic and copies ran while one was open for 0% of the time, Pallas kernels for 0%

commit v1 on v0

v1 whole, which is shorter than its diff:
```python
import jax
import jax.numpy as jnp
from jax import lax
from jax.sharding import PartitionSpec as P


def shards(database, query, slot_map, keys):
    rows_axis = lax.axis_size("row")
    cols_axis = lax.axis_size("col")
    factor = float(database.shape[0] * rows_axis) ** (-0.5)
    gathered = lax.all_gather(query, "col", axis=0, tiled=True)
    total, width = gathered.shape[0], database.shape[1]
    owned_count = total // (rows_axis * cols_axis)
    chosen = jnp.take(gathered, slot_map, axis=0)
    partial_value = jnp.dot(chosen, database, preferred_element_type=jnp.float32)
    blocks = partial_value.astype(jnp.bfloat16).reshape(rows_axis, -1, width)
    parts = lax.all_to_all(blocks, "row", split_axis=0, concat_axis=0, tiled=True)
    answers = jnp.sum(parts.astype(jnp.float32), axis=0)
    switched = (answers * factor).astype(jnp.bfloat16)
    owned = lax.all_to_all(switched, "col", split_axis=0, concat_axis=1, tiled=True)
    tiles = owned.reshape(owned_count, -1, keys.shape[1])
    return jnp.einsum("ptj,pjk->ptk", tiles, keys, preferred_element_type=jnp.float32)


def solution(mesh):
    placed = (P("row", "col"), P("col", "row"), P(), P(("row", "col"), None, None))
    return jax.shard_map(
        shards, mesh=mesh, in_specs=placed, out_specs=P(("row", "col"), None, None), check_vma=False
    )
```

time: 86.9 us -> 47.7 us (0.55)
  waiting for transfers between devices: 37.3 us -> 0 us
  between operations: 13.4 us -> 0.03 us
  blocking collectives: 25.3 us -> 38.6 us
  matrix products: 7.53 us -> 6.54 us
  other arithmetic: 2.3 us -> 1.41 us
    reduce_scatter x1 -> x0, waiting for transfers between devices: 37.3 us -> none  [shards(): lax.psum_scatter(partial_value, 'row', scatter_dimension=0, tiled=True)]
    all_to_all x1 -> x2, blocking collectives: 10.1 us -> 23.5 us  [the longest x1 13.2 us: shards(): lax.all_to_all(blocks, 'row', split_axis=0, concat_axis=0, tiled=True)]
    dot_general x1, matrix products: 4.07 us -> 3.08 us  [shards(): jnp.dot(chosen, database, preferred_element_type=jnp.float32)]
    convert_element_type x2 -> x1, other arithmetic: 0.97 us -> 0.01 us  [shards(): switched = (answers * factor).astype(jnp.bfloat16)]
  transfers between devices with their start and end apart: 1 -> 0, of which waited for: 1 -> 0; matrix products, arithmetic and copies ran while one was open for 0% -> 0% of each run, Pallas kernels for 0% -> 0%
where the time goes in v1:
time: 47.7 us; the launch traced here: 47.4 us
  blocking collectives  38.6 us (81%)
  matrix products  6.54 us (14%)
  other arithmetic  1.41 us (3%)
  local copies, waits for them, and re-layouts  0.83 us (2%)
    all_gather x1, blocking collectives, shards(): gathered = lax.all_gather(query, 'col', axis=0, tiled=True)  15.1 us
    all_to_all x1, blocking collectives, shards(): lax.all_to_all(blocks, 'row', split_axis=0, concat_axis=0, tiled=True)  13.2 us
    all_to_all x1, blocking collectives, shards(): lax.all_to_all(switched, 'col', split_axis=0, concat_axis=1, tiled=True)  10.3 us
    dot_general x1, matrix products, shards(): jnp.einsum('ptj,pjk->ptk', tiles, keys, preferred_element_type=jnp.float32)  3.46 us
    dot_general x1, matrix products, shards(): jnp.dot(chosen, database, preferred_element_type=jnp.float32)  3.08 us

profile of v1, /device:TPU:0, one launch (start us, length us, event | category | flops | bytes accessed | tf_op | source)
XLA Modules:
  0.0 47.4 jit_solution(14795891334420372258)
XLA Ops:
  0.0 0.7 %compare_and_fusion = pred[64]{0:T(512)(128)(4,1)S(1)} fusion(s32[64]{0:T(128)} %param.6), kind=kLoop, calls=%fused_computation.10 | loop fusion | flops 384 | bytes 320 | tf_op jit(solution)/shard_map/jit(_take)/and | solution.py:14
  0.7 0.7 %compare_select_fusion = s32[64]{0:T(128)S(1)} fusion(s32[64]{0:T(128)} %param.6), kind=kLoop, calls=%fused_computation.9 | loop fusion | flops 192 | bytes 512 | tf_op jit(solution)/shard_map/jit(_take)/jit(_where)/select_n | solution.py:14
  1.3 15.1 %all_gather.3 = bf16[64,512]{1,0:T(8,128)(2,1)S(1)} all-gather(bf16[16,512]{1,0:T(8,128)(2,1)} %param.5), channel_id=1, replica_groups=mesh['row'=8,'col'=4] {'col'}, dimensions={0}, use_global_device_ids=true | all-gather | bytes 81920 | tf_op jit(solution)/shard_map/all_gather | solution.py:11
  16.5 0.7 %gather_fusion = bf16[64,512]{1,0:T(8,128)(2,1)S(1)} fusion(bf16[64,512]{1,0:T(8,128)(2,1)S(1)} %all_gather.3, s32[1024]{0:T(1024)S(1)} %pad_clamp_fusion), kind=kCustom, calls=%fused_computation | custom fusion | bytes 131328 | tf_op jit(solution)/shard_map/jit(_take)/gather | solution.py:14
  17.2 3.1 %fusion = bf16[8,8,4096]{2,1,0:T(8,128)(2,1)S(1)} fusion(bf16[512,4096]{1,0:T(8,128)(2,1)} %param.4, bf16[64,512]{1,0:T(8,128)(2,1)S(1)} %gather_fusion, pred[64]{0:T(512)(128)(4,1)S(1)} %compare_and_fusion), kind=kOutput, calls=%fused_computation.2 | convolution fusion | flops 268730368 | bytes 4784192 | tf_op jit(solution)/shard_map/dot_general | solution.py:15
  20.2 13.2 %all_to_all.18 = bf16[8,8,4096]{2,1,0:T(8,128)(2,1)S(1)} all-to-all(bf16[8,8,4096]{2,1,0:T(8,128)(2,1)S(1)} %fusion), channel_id=1, replica_groups=mesh['row'=8,'col'=4] {'row'}, dimensions={0} | all-to-all | bytes 1048576 | tf_op jit(solution)/shard_map/all_to_all | solution.py:17
  33.5 0.1 convert_reduce_fusion
  33.6 0.1 convert_element_type.16
  33.6 10.3 %all_to_all.19 = bf16[4,2,4096]{2,1,0:T(2,128)(2,1)S(1)} all-to-all(bf16[4,2,4096]{2,1,0:T(2,128)(2,1)S(1)} %convert_element_type.16), channel_id=1, replica_groups=mesh['row'=8,'col'=4] {'col'}, dimensions={0} | all-to-all | bytes 131072 | tf_op jit(solution)/shard_map/all_to_all | solution.py:20
  43.9 0.1 copy.5
  44.0 3.5 %fusion.5 = f32[2,8,512]{2,1,0:T(8,128)} fusion(bf16[2,8,2048]{2,1,0:T(8,128)(2,1)S(1)} %reshape.20, bf16[2,2048,512]{2,1,0:T(8,128)(2,1)} %param.7), kind=kOutput, calls=%fused_computation.12 | convolution fusion | flops 33554432 | bytes 4292608 | tf_op jit(solution)/shard_map/ptj,pjk->ptk/dot_general | solution.py:22
  (3 shorter events, 0.0 us)

commit v2 on v1

v2 whole, which is shorter than its diff:
```python
import functools

import jax
import jax.numpy as jnp
from jax import lax
from jax.experimental import pallas as pl
from jax.experimental.pallas import tpu as pltpu
from jax.sharding import PartitionSpec as P


BF, F32 = jnp.bfloat16, jnp.float32
HBM = pl.BlockSpec(memory_space=pltpu.HBM)
VMEM = pl.BlockSpec(memory_space=pltpu.VMEM)
MIB = 1 << 20


def call(body, outs, ins, cost, scratch=(), limit=16 * MIB):
    return pl.pallas_call(
        body,
        out_shape=outs,
        in_specs=ins,
        out_specs=jax.tree.map(lambda _: VMEM, outs),
        scratch_shapes=list(scratch),
        compiler_params=pltpu.CompilerParams(vmem_limit_bytes=limit),
        cost_estimate=pl.CostEstimate(flops=cost[0], bytes_accessed=cost[1], transcendentals=0),
    )


def turn_order(rows):
    return sorted(range(1, rows // 2), key=lambda n: -n.bit_count())


def order_body(rows, cols, own, wanted_out, source_out):
    total = wanted_out.shape[0]
    each = total // (rows * cols)
    r, c = lax.axis_index("row"), lax.axis_index("col")
    i = lax.broadcasted_iota(jnp.int32, (total, total), 0)
    p = lax.broadcasted_iota(jnp.int32, (total, total), 1)
    group, rest = lax.div(i, cols * each), lax.rem(i, cols * each)
    step, lane = lax.div(rest, each), lax.rem(rest, each)
    half = rows // 2
    turn = jnp.where(group < half, 2 * group, 2 * (group - half) + 1)
    slot = ((turn ^ r) * cols + (step ^ c)) * each + lane
    wanted_out[...] = jnp.where(slot == p, 1.0, 0.0).astype(BF)
    source_out[...] = (c ^ lax.div(i, own)) * own + lax.rem(i, own)


def product_body(pieces, wanted, source, slots, *refs):
    queries, (database, keep, send) = refs[:pieces], refs[pieces:]
    served = jnp.where(slots[...] == source[...], 1.0, 0.0).astype(BF)
    pick = lax.dot_general(
        wanted[...], served, (((1,), (1,)), ((), ())), preferred_element_type=F32
    ).astype(BF)
    gathered = jnp.concatenate([q[...] for q in queries], axis=0)
    chosen = jnp.dot(pick, gathered, preferred_element_type=F32).astype(BF)
    half = keep.shape[0]
    value = jnp.dot(chosen, database[...], preferred_element_type=F32)
    keep[...] = value[:half]
    send[...] = value[half:].astype(BF)


def halve_body(keep, got, own, *sends):
    rows = own.shape[0]
    own[...] = keep[:rows] + got[:rows].astype(F32)
    for n, out in enumerate(sends, 1):
        part = slice(n * rows, (n + 1) * rows)
        out[...] = (keep[part] + got[part].astype(F32)).astype(BF)


def switch_body(factor, arrivals, own, *refs):
    got, outs = refs[:arrivals], refs[arrivals:]
    value = own[...]
    for ref in got:
        value = value + ref[...].astype(F32)
    switched = (value * factor).astype(F32)
    each = outs[0].shape[0]
    for n, out in enumerate(outs):
        out[...] = switched[n * each : (n + 1) * each].astype(BF)


def pack_body(cols, *refs):
    got, (keys, out, tiles) = refs[:cols], refs[cols:]
    count, depth = keys.shape[0], keys.shape[1]
    per = got[0].shape[1] // depth
    c = lax.axis_index("col")
    for s in range(count):
        for k in range(cols):
            source = c ^ k
            for h in range(per):
                row = got[k][s : s + 1, h * depth : (h + 1) * depth].astype(F32)
                tiles[s, pl.ds(source * per + h, 1), :] = row
        out[s] = jnp.dot(tiles[s].astype(BF), keys[s], preferred_element_type=F32)


def shards(database, query, slot_map, keys):
    rows, cols = lax.axis_size("row"), lax.axis_size("col")
    own, depth = query.shape
    width = database.shape[1]
    total = own * cols
    each = total // (rows * cols)
    half, block = total // 2, total // rows
    factor = float(depth * rows) ** (-0.5)
    S = jax.ShapeDtypeStruct

    def along_row(x, k):
        return lax.ppermute(x, "row", [(i, i ^ k) for i in range(rows)])

    def along_col(x, k):
        return lax.ppermute(x, "col", [(i, i ^ k) for i in range(cols)])

    hops = range(1, cols)
    arrived = dict((k, along_col(query, k)) for k in hops)
    wanted, source = call(
        functools.partial(order_body, rows, cols, own),
        (S((total, total), BF), S((total, total), jnp.int32)),
        [],
        (10**10, 10 * MIB),
    )()
    keep, send = call(
        functools.partial(product_body, cols),
        (S((half, width), F32), S((half, width), BF)),
        [VMEM] * (cols + 4),
        (2 * total * depth * width, database.size * 2),
    )(wanted, source, slot_map.reshape(1, total), query, *[arrived[k] for k in range(1, cols)], database)
    got = along_row(send, 1)
    kept, *sends = call(
        halve_body,
        [S((block, width), F32)] + [S((block, width), BF)] * (rows // 2 - 1),
        [VMEM, VMEM],
        (half * width, half * width * 6),
    )(keep, got)
    turns = turn_order(rows)
    swapped = [along_row(sends[n - 1], 2 * n) for n in turns]
    outs = call(
        functools.partial(switch_body, factor, rows // 2 - 1),
        [S((each, width), BF)] * cols,
        [VMEM] * (rows // 2),
        (block * width * rows, block * width * 8),
    )(kept, *swapped)
    moved = dict((k, along_col(outs[k], k)) for k in range(1, cols))
    blocks = [outs[0]] + [moved[k] for k in range(1, cols)]
    tiles = cols * width // keys.shape[1]
    return call(
        functools.partial(pack_body, cols),
        S((each, tiles, keys.shape[2]), F32),
        [VMEM] * (cols + 1),
        (2 * each * tiles * keys.shape[1] * keys.shape[2], keys.size * 2),
        [pltpu.VMEM((each, tiles, keys.shape[1]), F32)],
    )(*blocks, keys)


def solution(mesh):
    placed = (P("row", "col"), P("col", "row"), P(), P(("row", "col"), None, None))
    return jax.shard_map(
        shards, mesh=mesh, in_specs=placed, out_specs=P(("row", "col"), None, None), check_vma=False
    )
```

time: 47.7 us -> 29.4 us (0.62)
  blocking collectives: 38.6 us -> 0 us
  starting transfers between devices: 0 us -> 13.8 us
  waiting for transfers between devices: 0 us -> 12.9 us
  matrix products: 6.54 us -> 0 us
  Pallas kernels: 0 us -> 2.47 us
  other arithmetic: 1.41 us -> 0 us
  local copies, waits for them, and re-layouts: 0.83 us -> 0.02 us
    all_to_all x2 -> x0, blocking collectives: 23.5 us -> none  [the longest x1 13.2 us: shards(): lax.all_to_all(blocks, 'row', split_axis=0, concat_axis=0, tiled=True)]
    all_gather x1 -> x0, blocking collectives: 15.1 us -> none  [shards(): gathered = lax.all_gather(query, 'col', axis=0, tiled=True)]
    ppermute x0 -> x10, starting transfers between devices: none -> 13.8 us  [the longest x6 10.2 us: along_col(): return lax.ppermute(x, 'col', [(i, i ^ k) for i in range(cols)])]
    ppermute x0 -> x10, waiting for transfers between devices: none -> 12.9 us  [the longest x6 7.63 us: along_col(): return lax.ppermute(x, 'col', [(i, i ^ k) for i in range(cols)])]
    dot_general x2 -> x0, matrix products: 6.54 us -> none  [the longest x1 3.46 us: shards(): jnp.einsum('ptj,pjk->ptk', tiles, keys, preferred_element_type=jnp.float32)]
    pallas_call x0 -> x5, Pallas kernels: none -> 2.47 us  [the longest x1 1.28 us: shards(): call(functools.partial(pack_body, cols), S((each, tiles, keys.shape[2]),...]
    gather x1 -> x0, local copies, waits for them, and re-layouts: 0.7 us -> none  [shards(): chosen = jnp.take(gathered, slot_map, axis=0)]
    and x1 -> x0, other arithmetic: 0.66 us -> none  [shards(): chosen = jnp.take(gathered, slot_map, axis=0)]
  transfers between devices with their start and end apart: 0 -> 10, of which waited for: 0 -> 9; matrix products, arithmetic and copies ran while one was open for 0% -> 0% of each run, Pallas kernels for 0% -> 0%
where the time goes in v2:
time: 29.4 us; the launch traced here: 29.2 us
  starting transfers between devices  13.8 us (47%)
  waiting for transfers between devices  12.9 us (44%)
  Pallas kernels  2.47 us (8%)
    ppermute x6, starting transfers between devices, along_col(): return lax.ppermute(x, 'col', [(i, i ^ k) for i in range(cols)])  10.2 us
    ppermute x6, waiting for transfers between devices, along_col(): return lax.ppermute(x, 'col', [(i, i ^ k) for i in range(cols)])  7.63 us
    ppermute x4, waiting for transfers between devices, along_row(): return lax.ppermute(x, 'row', [(i, i ^ k) for i in range(rows)])  5.28 us
    ppermute x4, starting transfers between devices, along_row(): return lax.ppermute(x, 'row', [(i, i ^ k) for i in range(rows)])  3.62 us
    pallas_call x1, Pallas kernels, shards(): call(functools.partial(pack_body, cols), S((each, tiles, keys.shape[2]),...  1.28 us
    pallas_call x1, Pallas kernels, shards(): call(functools.partial(product_body, cols), (S((half, width), F32), S((ha...  1.07 us
  transfers between devices with their start and end apart: 10, of which 9 were waited for; matrix products, arithmetic and copies ran while one was open for 0% of the time, Pallas kernels for 0%

profile of v2, /device:TPU:0, one launch (start us, length us, event | category | flops | bytes accessed | tf_op | source)
XLA Modules:
  0.0 29.2 jit_solution(14608632803237500295)
XLA Ops:
  0.0 0.0 copy-start.2
  0.0 0.0 copy-start.3
  0.0 0.0 copy-start
  0.0 4.1 %collective-permute-start.1 = (bf16[16,512]{1,0:T(8,128)(2,1)}, bf16[16,512]{1,0:T(8,128)(2,1)S(1)}, u32[]{:S(2)}, u32[]{:S(2)}) collective-permute-start(bf16[16,512]{1,0:T(8,128)(2,1)} %refs_0_.1), channel_id=1, source_target_pairs={{0,2},{1,3},{2,0},{3,1},{4,6},{5,7},{6,4},{7,5},{8,10},{9,11},{10,... | collective-permute-start | bytes 49160 | tf_op jit(solution)/shard_map/ppermute | solution.py:109
  4.1 1.6 %collective-permute-start = (bf16[16,512]{1,0:T(8,128)(2,1)}, bf16[16,512]{1,0:T(8,128)(2,1)S(1)}, u32[]{:S(2)}, u32[]{:S(2)}) collective-permute-start(bf16[16,512]{1,0:T(8,128)(2,1)} %refs_0_.1), channel_id=1, source_target_pairs={{0,1},{1,0},{2,3},{3,2},{4,5},{5,4},{6,7},{7,6},{8,9},{9,8},{10,11... | collective-permute-start | bytes 49160 | tf_op jit(solution)/shard_map/ppermute | solution.py:109
  5.7 0.0 collective-permute-start.2
  5.8 0.0 copy-start.1
  5.8 0.3 %collective-permute-done.1.refs_2_ = bf16[16,512]{1,0:T(8,128)(2,1)S(1)} collective-permute-done((bf16[16,512]{1,0:T(8,128)(2,1)}, bf16[16,512]{1,0:T(8,128)(2,1)S(1)}, u32[]{:S(2)}, u32[]{:S(2)}) %collective-permute-start.1) | collective-permute-done | bytes 16416 | tf_op jit(solution)/shard_map/ppermute | solution.py:109
  6.1 2.0 %collective-permute-done.refs_1_ = bf16[16,512]{1,0:T(8,128)(2,1)S(1)} collective-permute-done((bf16[16,512]{1,0:T(8,128)(2,1)}, bf16[16,512]{1,0:T(8,128)(2,1)S(1)}, u32[]{:S(2)}, u32[]{:S(2)}) %collective-permute-start) | collective-permute-done | bytes 16416 | tf_op jit(solution)/shard_map/ppermute | solution.py:109
  8.1 3.4 %collective-permute-done.2.refs_3_ = bf16[16,512]{1,0:T(8,128)(2,1)S(1)} collective-permute-done((bf16[16,512]{1,0:T(8,128)(2,1)}, bf16[16,512]{1,0:T(8,128)(2,1)S(1)}, u32[]{:S(2)}, u32[]{:S(2)}) %collective-permute-start.2) | collective-permute-done | bytes 16416 | tf_op jit(solution)/shard_map/ppermute | solution.py:109
  11.5 0.0 copy-done.2
  11.5 0.0 copy-done.3
  11.5 0.0 copy-done
  11.5 1.1 %shard_map.47 = (f32[32,4096]{1,0:T(8,128)S(1)}, bf16[32,4096]{1,0:T(8,128)(2,1)S(1)}) custom-call(bf16[64,64]{1,0:T(8,128)(2,1)S(1)} %get-tuple-element.17.wanted, s32[64,64]{1,0:T(8,128)S(1)} %get-tuple-element.18.source, s32[1,64]{1,0:T(1,128)S(1)} %bitcast.1, bf16[16,512]{1,0:T(8,128)(2,1)S(1)} %copy-done.2, ...), custom_call_target="tpu_custom_call" | custom-call | flops 268435456 | bytes 4194304 | tf_op jit(solution)/shard_map/pallas_call | solution.py:119
  12.6 0.1 collective-permute-start.3
  12.6 1.5 %collective-permute-done.3.got = bf16[32,4096]{1,0:T(8,128)(2,1)S(1)} collective-permute-done((bf16[32,4096]{1,0:T(8,128)(2,1)S(1)}, bf16[32,4096]{1,0:T(8,128)(2,1)S(1)}, u32[]{:S(2)}, u32[]{:S(2)}) %collective-permute-start.3) | collective-permute-done | bytes 262176 | tf_op jit(solution)/shard_map/ppermute | solution.py:106
  14.2 2.5 %collective-permute-start.4 = (bf16[8,4096]{1,0:T(8,128)(2,1)S(1)}, bf16[8,4096]{1,0:T(8,128)(2,1)S(1)}, u32[]{:S(2)}, u32[]{:S(2)}) collective-permute-start(bf16[8,4096]{1,0:T(8,128)(2,1)S(1)} %get-tuple-element.22), channel_id=1, source_target_pairs={{0,24},{4,28},{8,16},{12,20},{16,8},{20,12},{24,0},{28,4},{1,25},{... | collective-permute-start | bytes 196616 | tf_op jit(solution)/shard_map/ppermute | solution.py:106
  16.7 0.5 %collective-permute-start.5 = (bf16[8,4096]{1,0:T(8,128)(2,1)S(1)}, bf16[8,4096]{1,0:T(8,128)(2,1)S(1)}, u32[]{:S(2)}, u32[]{:S(2)}) collective-permute-start(bf16[8,4096]{1,0:T(8,128)(2,1)S(1)} %get-tuple-element.23), channel_id=1, source_target_pairs={{0,8},{4,12},{8,0},{12,4},{16,24},{20,28},{24,16},{28,20},{1,9},{5... | collective-permute-start | bytes 196616 | tf_op jit(solution)/shard_map/ppermute | solution.py:106
  17.3 0.5 %collective-permute-start.6 = (bf16[8,4096]{1,0:T(8,128)(2,1)S(1)}, bf16[8,4096]{1,0:T(8,128)(2,1)S(1)}, u32[]{:S(2)}, u32[]{:S(2)}) collective-permute-start(bf16[8,4096]{1,0:T(8,128)(2,1)S(1)} %get-tuple-element.24), channel_id=1, source_target_pairs={{0,16},{4,20},{8,24},{12,28},{16,0},{20,4},{24,8},{28,12},{1,17},{... | collective-permute-start | bytes 196616 | tf_op jit(solution)/shard_map/ppermute | solution.py:106
  17.8 2.0 %collective-permute-done.4.refs_0_ = bf16[8,4096]{1,0:T(8,128)(2,1)S(1)} collective-permute-done((bf16[8,4096]{1,0:T(8,128)(2,1)S(1)}, bf16[8,4096]{1,0:T(8,128)(2,1)S(1)}, u32[]{:S(2)}, u32[]{:S(2)}) %collective-permute-start.4) | collective-permute-done | bytes 65568 | tf_op jit(solution)/shard_map/ppermute | solution.py:106
  19.8 1.2 %collective-permute-done.5.refs_1_ = bf16[8,4096]{1,0:T(8,128)(2,1)S(1)} collective-permute-done((bf16[8,4096]{1,0:T(8,128)(2,1)S(1)}, bf16[8,4096]{1,0:T(8,128)(2,1)S(1)}, u32[]{:S(2)}, u32[]{:S(2)}) %collective-permute-start.5) | collective-permute-done | bytes 65568 | tf_op jit(solution)/shard_map/ppermute | solution.py:106
  21.0 0.5 %collective-permute-done.6.refs_2_ = bf16[8,4096]{1,0:T(8,128)(2,1)S(1)} collective-permute-done((bf16[8,4096]{1,0:T(8,128)(2,1)S(1)}, bf16[8,4096]{1,0:T(8,128)(2,1)S(1)}, u32[]{:S(2)}, u32[]{:S(2)}) %collective-permute-start.6) | collective-permute-done | bytes 65568 | tf_op jit(solution)/shard_map/ppermute | solution.py:106
  21.6 0.1 collective-permute-start.7
  21.6 0.8 %collective-permute-start.8 = (bf16[2,4096]{1,0:T(2,128)(2,1)S(1)}, bf16[2,4096]{1,0:T(2,128)(2,1)S(1)}, u32[]{:S(2)}, u32[]{:S(2)}) collective-permute-start(bf16[2,4096]{1,0:T(2,128)(2,1)S(1)} %get-tuple-element.27), channel_id=1, source_target_pairs={{0,2},{1,3},{2,0},{3,1},{4,6},{5,7},{6,4},{7,5},{8,10},{9,11},{10,... | collective-permute-start | bytes 49160 | tf_op jit(solution)/shard_map/ppermute | solution.py:109
  22.4 3.6 %collective-permute-start.9 = (bf16[2,4096]{1,0:T(2,128)(2,1)S(1)}, bf16[2,4096]{1,0:T(2,128)(2,1)S(1)}, u32[]{:S(2)}, u32[]{:S(2)}) collective-permute-start(bf16[2,4096]{1,0:T(2,128)(2,1)S(1)} %get-tuple-element.28), channel_id=1, source_target_pairs={{0,3},{1,2},{2,1},{3,0},{4,7},{5,6},{6,5},{7,4},{8,11},{9,10},{10,... | collective-permute-start | bytes 49160 | tf_op jit(solution)/shard_map/ppermute | solution.py:109
  26.0 0.0 collective-permute-done.7.refs_1_
  26.0 0.3 %collective-permute-done.8.refs_2_ = bf16[2,4096]{1,0:T(2,128)(2,1)S(1)} collective-permute-done((bf16[2,4096]{1,0:T(2,128)(2,1)S(1)}, bf16[2,4096]{1,0:T(2,128)(2,1)S(1)}, u32[]{:S(2)}, u32[]{:S(2)}) %collective-permute-start.8) | collective-permute-done | bytes 16416 | tf_op jit(solution)/shard_map/ppermute | solution.py:109
  26.4 1.6 %collective-permute-done.9.refs_3_ = bf16[2,4096]{1,0:T(2,128)(2,1)S(1)} collective-permute-done((bf16[2,4096]{1,0:T(2,128)(2,1)S(1)}, bf16[2,4096]{1,0:T(2,128)(2,1)S(1)}, u32[]{:S(2)}, u32[]{:S(2)}) %collective-permute-start.9) | collective-permute-done | bytes 16416 | tf_op jit(solution)/shard_map/ppermute | solution.py:109
  28.0 0.0 copy-done.1
  28.0 1.3 %shard_map.50 = f32[2,8,512]{2,1,0:T(8,128)} custom-call(bf16[2,4096]{1,0:T(2,128)(2,1)S(1)} %get-tuple-element.25.refs_0_, bf16[2,4096]{1,0:T(2,128)(2,1)S(1)} %collective-permute-done.7.refs_1_, bf16[2,4096]{1,0:T(2,128)(2,1)S(1)} %collective-permute-done.8.refs_2_, bf16[2,4096]{1,0:T(2,128)(2,1)S(1)} %collective-permute-done.9.refs_3_, ...), custom_call_target="tpu_custom_call" | custom-call | flops 33554432 | bytes 4194304 | tf_op jit(solution)/shard_map/pallas_call | solution.py:143
  (3 shorter events, 0.1 us)
Async XLA Ops:
  0.0 11.5 %copy-start.2 = (bf16[16,512]{1,0:T(8,128)(2,1)S(1)}, bf16[16,512]{1,0:T(8,128)(2,1)}, u32[]{:S(2)}) copy-start(bf16[16,512]{1,0:T(8,128)(2,1)} %refs_0_.1) | copy-start | bytes 49156
  0.0 11.5 %copy-start.3 = (s32[64]{0:T(128)S(1)}, s32[64]{0:T(128)}, u32[]{:S(2)}) copy-start(s32[64]{0:T(128)} %param.6) | copy-start | bytes 772
  0.0 11.5 %copy-start = (bf16[512,4096]{1,0:T(8,128)(2,1)S(1)}, bf16[512,4096]{1,0:T(8,128)(2,1)}, u32[]{:S(2)}) copy-start(bf16[512,4096]{1,0:T(8,128)(2,1)} %refs_4_.2) | copy-start | bytes 12582916
  0.0 6.1 %collective-permute-start.1 = (bf16[16,512]{1,0:T(8,128)(2,1)}, bf16[16,512]{1,0:T(8,128)(2,1)S(1)}, u32[]{:S(2)}, u32[]{:S(2)}) collective-permute-start(bf16[16,512]{1,0:T(8,128)(2,1)} %refs_0_.1), channel_id=1, source_target_pairs={{0,2},{1,3},{2,0},{3,1},{4,6},{5,7},{6,4},{7,5},{8,10},{9,11},{10,... | collective-permute-start | bytes 49160 | tf_op jit(solution)/shard_map/ppermute | solution.py:109
  4.1 3.9 %collective-permute-start = (bf16[16,512]{1,0:T(8,128)(2,1)}, bf16[16,512]{1,0:T(8,128)(2,1)S(1)}, u32[]{:S(2)}, u32[]{:S(2)}) collective-permute-start(bf16[16,512]{1,0:T(8,128)(2,1)} %refs_0_.1), channel_id=1, source_target_pairs={{0,1},{1,0},{2,3},{3,2},{4,5},{5,4},{6,7},{7,6},{8,9},{9,8},{10,11... | collective-permute-start | bytes 49160 | tf_op jit(solution)/shard_map/ppermute | solution.py:109
  5.7 5.7 %collective-permute-start.2 = (bf16[16,512]{1,0:T(8,128)(2,1)}, bf16[16,512]{1,0:T(8,128)(2,1)S(1)}, u32[]{:S(2)}, u32[]{:S(2)}) collective-permute-start(bf16[16,512]{1,0:T(8,128)(2,1)} %refs_0_.1), channel_id=1, source_target_pairs={{0,3},{1,2},{2,1},{3,0},{4,7},{5,6},{6,5},{7,4},{8,11},{9,10},{10,... | collective-permute-start | bytes 49160 | tf_op jit(solution)/shard_map/ppermute | solution.py:109
  5.8 22.2 %copy-start.1 = (bf16[2,2048,512]{2,1,0:T(8,128)(2,1)S(1)}, bf16[2,2048,512]{2,1,0:T(8,128)(2,1)}, u32[]{:S(2)}) copy-start(bf16[2,2048,512]{2,1,0:T(8,128)(2,1)} %refs_4_.3) | copy-start | bytes 12582916
  12.6 1.6 %collective-permute-start.3 = (bf16[32,4096]{1,0:T(8,128)(2,1)S(1)}, bf16[32,4096]{1,0:T(8,128)(2,1)S(1)}, u32[]{:S(2)}, u32[]{:S(2)}) collective-permute-start(bf16[32,4096]{1,0:T(8,128)(2,1)S(1)} %get-tuple-element.20), channel_id=1, source_target_pairs={{0,4},{4,0},{8,12},{12,8},{16,20},{20,16},{24,28},{28,24},{1,5},{5... | collective-permute-start | bytes 786440 | tf_op jit(solution)/shard_map/ppermute | solution.py:106
  14.2 5.6 %collective-permute-start.4 = (bf16[8,4096]{1,0:T(8,128)(2,1)S(1)}, bf16[8,4096]{1,0:T(8,128)(2,1)S(1)}, u32[]{:S(2)}, u32[]{:S(2)}) collective-permute-start(bf16[8,4096]{1,0:T(8,128)(2,1)S(1)} %get-tuple-element.22), channel_id=1, source_target_pairs={{0,24},{4,28},{8,16},{12,20},{16,8},{20,12},{24,0},{28,4},{1,25},{... | collective-permute-start | bytes 196616 | tf_op jit(solution)/shard_map/ppermute | solution.py:106
  16.7 4.3 %collective-permute-start.5 = (bf16[8,4096]{1,0:T(8,128)(2,1)S(1)}, bf16[8,4096]{1,0:T(8,128)(2,1)S(1)}, u32[]{:S(2)}, u32[]{:S(2)}) collective-permute-start(bf16[8,4096]{1,0:T(8,128)(2,1)S(1)} %get-tuple-element.23), channel_id=1, source_target_pairs={{0,8},{4,12},{8,0},{12,4},{16,24},{20,28},{24,16},{28,20},{1,9},{5... | collective-permute-start | bytes 196616 | tf_op jit(solution)/shard_map/ppermute | solution.py:106
  17.3 4.3 %collective-permute-start.6 = (bf16[8,4096]{1,0:T(8,128)(2,1)S(1)}, bf16[8,4096]{1,0:T(8,128)(2,1)S(1)}, u32[]{:S(2)}, u32[]{:S(2)}) collective-permute-start(bf16[8,4096]{1,0:T(8,128)(2,1)S(1)} %get-tuple-element.24), channel_id=1, source_target_pairs={{0,16},{4,20},{8,24},{12,28},{16,0},{20,4},{24,8},{28,12},{1,17},{... | collective-permute-start | bytes 196616 | tf_op jit(solution)/shard_map/ppermute | solution.py:106
  21.6 4.5 %collective-permute-start.7 = (bf16[2,4096]{1,0:T(2,128)(2,1)S(1)}, bf16[2,4096]{1,0:T(2,128)(2,1)S(1)}, u32[]{:S(2)}, u32[]{:S(2)}) collective-permute-start(bf16[2,4096]{1,0:T(2,128)(2,1)S(1)} %get-tuple-element.26), channel_id=1, source_target_pairs={{0,1},{1,0},{2,3},{3,2},{4,5},{5,4},{6,7},{7,6},{8,9},{9,8},{10,11... | collective-permute-start | bytes 49160 | tf_op jit(solution)/shard_map/ppermute | solution.py:109
  21.6 4.7 %collective-permute-start.8 = (bf16[2,4096]{1,0:T(2,128)(2,1)S(1)}, bf16[2,4096]{1,0:T(2,128)(2,1)S(1)}, u32[]{:S(2)}, u32[]{:S(2)}) collective-permute-start(bf16[2,4096]{1,0:T(2,128)(2,1)S(1)} %get-tuple-element.27), channel_id=1, source_target_pairs={{0,2},{1,3},{2,0},{3,1},{4,6},{5,7},{6,4},{7,5},{8,10},{9,11},{10,... | collective-permute-start | bytes 49160 | tf_op jit(solution)/shard_map/ppermute | solution.py:109
  22.4 5.5 %collective-permute-start.9 = (bf16[2,4096]{1,0:T(2,128)(2,1)S(1)}, bf16[2,4096]{1,0:T(2,128)(2,1)S(1)}, u32[]{:S(2)}, u32[]{:S(2)}) collective-permute-start(bf16[2,4096]{1,0:T(2,128)(2,1)S(1)} %get-tuple-element.28), channel_id=1, source_target_pairs={{0,3},{1,2},{2,1},{3,0},{4,7},{5,6},{6,5},{7,4},{8,11},{9,10},{10,... | collective-permute-start | bytes 49160 | tf_op jit(solution)/shard_map/ppermute | solution.py:109

commit v3 on v2

v3 whole, which is shorter than its diff:
```python
import functools

import jax
import jax.numpy as jnp
from jax import lax
from jax.experimental import pallas as pl
from jax.experimental.pallas import tpu as pltpu
from jax.sharding import PartitionSpec as P


BF, F32 = jnp.bfloat16, jnp.float32
VMEM = pl.BlockSpec(memory_space=pltpu.VMEM)
MIB = 1 << 20
COVER = 10**10


def call(body, outs, operands, flops, nbytes, scratch=()):
    return pl.pallas_call(
        body,
        out_shape=outs,
        in_specs=[VMEM] * len(operands),
        out_specs=jax.tree.map(lambda _: VMEM, outs),
        scratch_shapes=list(scratch),
        compiler_params=pltpu.CompilerParams(vmem_limit_bytes=16 * MIB),
        cost_estimate=pl.CostEstimate(flops=flops, bytes_accessed=nbytes, transcendentals=0),
    )(*operands)


def lookup(table, index):
    out = jnp.full_like(index, table[0])
    for n, value in enumerate(table[1:], 1):
        out = jnp.where(index == n, value, out)
    return out


def ring_of(cols):
    return [i ^ (i >> 1) for i in range(cols)]


def turns_of(rows):
    return [2 * n for n in sorted(range(1, rows // 2), key=lambda n: -n.bit_count())] + [0]


def order_body(rows, cols, own, wanted, source):
    total = wanted.shape[0]
    each = total // (rows * cols)
    r, c = lax.axis_index("row"), lax.axis_index("col")
    i = lax.broadcasted_iota(jnp.int32, (total, total), 0)
    p = lax.broadcasted_iota(jnp.int32, (total, total), 1)
    group, rest = lax.div(i, cols * each), lax.rem(i, cols * each)
    step, lane = lax.div(rest, each), lax.rem(rest, each)
    turns = turns_of(rows)
    turn = lookup(turns + [t + 1 for t in turns], group)
    slot = ((turn ^ r) * cols + (step ^ c)) * each + lane
    wanted[...] = jnp.where(slot == p, 1.0, 0.0).astype(BF)
    ring = ring_of(cols)
    place = lookup([ring.index(n) for n in range(cols)], c + 0 * i)
    origin = lookup(ring, lax.rem(place - lax.div(i, own) + cols, cols))
    source[...] = origin * own + lax.rem(i, own)


def pick_body(wanted, source, slots, pick):
    served = jnp.where(slots[...] == source[...], 1.0, 0.0).astype(BF)
    pick[...] = lax.dot_general(
        wanted[...], served, (((1,), (1,)), ((), ())), preferred_element_type=F32
    ).astype(BF)


def product_body(pieces, pick, *refs):
    queries, (database, keep, first, rest) = refs[:pieces], refs[pieces:]
    gathered = jnp.concatenate([q[...] for q in queries], axis=0)
    chosen = jnp.dot(pick[...], gathered, preferred_element_type=F32).astype(BF)
    half, block = keep.shape[0], first.shape[0]
    value = jnp.dot(chosen, database[...], preferred_element_type=F32)
    keep[...] = value[:half]
    first[...] = value[half : half + block].astype(BF)
    rest[...] = value[half + block :].astype(BF)


def first_body(keep, got, out):
    out[...] = (keep[: out.shape[0]] + got[...].astype(F32)).astype(BF)


def rest_body(keep, got, *outs):
    rows = outs[0].shape[0]
    for n, out in enumerate(outs):
        value = keep[(n + 1) * rows : (n + 2) * rows] + got[n * rows : (n + 1) * rows].astype(F32)
        out[...] = value.astype(out.dtype)


def switch_body(factor, arrivals, own, *refs):
    got, outs = refs[:arrivals], refs[arrivals:]
    value = own[...]
    for ref in got:
        value = value + ref[...].astype(F32)
    switched = value * factor
    each = outs[0].shape[0]
    for n, out in enumerate(outs):
        out[...] = switched[n * each : (n + 1) * each].astype(BF)


def pack_body(cols, *refs):
    got, (keys, out, tiles) = refs[:cols], refs[cols:]
    count, depth = keys.shape[0], keys.shape[1]
    per = got[0].shape[1] // depth
    c = lax.axis_index("col")
    for s in range(count):
        for k in range(cols):
            for h in range(per):
                row = got[k][s : s + 1, h * depth : (h + 1) * depth].astype(F32)
                tiles[s, pl.ds((c ^ k) * per + h, 1), :] = row
        out[s] = jnp.dot(tiles[s].astype(BF), keys[s], preferred_element_type=F32)


def shards(database, query, slot_map, keys):
    rows, cols = lax.axis_size("row"), lax.axis_size("col")
    own, depth = query.shape
    width = database.shape[1]
    total = own * cols
    each = total // (rows * cols)
    half, block = total // 2, total // rows
    factor = float(depth * rows) ** (-0.5)
    S = jax.ShapeDtypeStruct
    ring, turns = ring_of(cols), turns_of(rows)

    def along_row(x, k):
        return lax.ppermute(x, "row", [(i, i ^ k) for i in range(rows)])

    arrived = [
        lax.ppermute(query, "col", [(ring[i], ring[(i + k) % cols]) for i in range(cols)])
        for k in range(1, cols)
    ]
    wanted, source = call(
        functools.partial(order_body, rows, cols, own),
        [S((total, total), BF), S((total, total), jnp.int32)],
        [],
        COVER,
        8 * total * total,
    )
    pick = call(
        pick_body,
        S((total, total), BF),
        [wanted, source, slot_map.reshape(1, total)],
        2 * total**3,
        8 * total * total,
    )
    keep, first, rest = call(
        functools.partial(product_body, cols),
        [S((half, width), F32), S((block, width), BF), S((half - block, width), BF)],
        [pick, query, *arrived, database],
        2 * total * depth * width,
        database.size * 2,
    )
    first = along_row(first, 1)
    rest = along_row(rest, 1)
    lead = call(first_body, S((block, width), BF), [keep, first], block * width, 8 * block * width)
    lead = along_row(lead, turns[0])
    *others, kept = call(
        rest_body,
        [S((block, width), BF)] * (rows // 2 - 2) + [S((block, width), F32)],
        [keep, rest],
        half * width,
        6 * half * width,
    )
    swapped = [lead] + [along_row(x, turns[n]) for n, x in enumerate(others, 1)]
    outs = call(
        functools.partial(switch_body, factor, len(swapped)),
        [S((each, width), BF)] * cols,
        [kept, *swapped],
        block * width * rows,
        8 * block * width,
    )
    blocks = [outs[0]] + [
        lax.ppermute(outs[k], "col", [(i, i ^ k) for i in range(cols)])
        for k in range(1, cols)
    ]
    tiles = cols * width // keys.shape[1]
    return call(
        functools.partial(pack_body, cols),
        S((each, tiles, keys.shape[2]), F32),
        [*blocks, keys],
        2 * each * tiles * keys.shape[1] * keys.shape[2],
        keys.size * 2,
        [pltpu.VMEM((each, tiles, keys.shape[1]), F32)],
    )


def solution(mesh):
    placed = (P("row", "col"), P("col", "row"), P(), P(("row", "col"), None, None))
    return jax.shard_map(
        shards, mesh=mesh, in_specs=placed, out_specs=P(("row", "col"), None, None), check_vma=False
    )
```

time: 29.4 us -> 30.1 us (1.024)
  starting transfers between devices: 13.8 us -> 16.7 us
  waiting for transfers between devices: 12.9 us -> 10.7 us
    ppermute x6, starting transfers between devices: 10.2 us -> 12.5 us  [the longest x3 8.07 us: shards(): lax.ppermute(query, 'col', [(ring[i], ring[(i + k) % cols]) for i in rang...]
    ppermute x6, waiting for transfers between devices: 7.63 us -> 6.05 us  [the longest x3 4.15 us: shards(): lax.ppermute(outs[k], 'col', [(i, i ^ k) for i in range(cols)])]
    ppermute x4 -> x5, waiting for transfers between devices: 5.28 us -> 4.61 us  [along_row(): return lax.ppermute(x, 'row', [(i, i ^ k) for i in range(rows)])]
    ppermute x4 -> x5, starting transfers between devices: 3.62 us -> 4.19 us  [along_row(): return lax.ppermute(x, 'row', [(i, i ^ k) for i in range(rows)])]
    pallas_call x5 -> x7, Pallas kernels: 2.47 us -> 2.48 us  [call(): pl.pallas_call(body, out_shape=outs, in_specs=[VMEM] * len(operands), out...]
  transfers between devices with their start and end apart: 10 -> 11, of which waited for: 9 -> 7; matrix products, arithmetic and copies ran while one was open for 0% -> 0% of each run, Pallas kernels for 0% -> 1%
where the time goes in v3:
time: 30.1 us; the launch traced here: 29.9 us
  starting transfers between devices  16.7 us (55%)
  waiting for transfers between devices  10.7 us (36%)
  Pallas kernels  2.48 us (8%)
    ppermute x3, starting transfers between devices, shards(): lax.ppermute(query, 'col', [(ring[i], ring[(i + k) % cols]) for i in rang...  8.07 us
    ppermute x5, waiting for transfers between devices, along_row(): return lax.ppermute(x, 'row', [(i, i ^ k) for i in range(rows)])  4.61 us
    ppermute x3, starting transfers between devices, shards(): lax.ppermute(outs[k], 'col', [(i, i ^ k) for i in range(cols)])  4.45 us
    ppermute x5, starting transfers between devices, along_row(): return lax.ppermute(x, 'row', [(i, i ^ k) for i in range(rows)])  4.19 us
    ppermute x3, waiting for transfers between devices, shards(): lax.ppermute(outs[k], 'col', [(i, i ^ k) for i in range(cols)])  4.15 us
    pallas_call x7, Pallas kernels, call(): pl.pallas_call(body, out_shape=outs, in_specs=[VMEM] * len(operands), out...  2.48 us
    ppermute x3, waiting for transfers between devices, shards(): lax.ppermute(query, 'col', [(ring[i], ring[(i + k) % cols]) for i in rang...  1.91 us
  transfers between devices with their start and end apart: 11, of which 7 were waited for; matrix products, arithmetic and copies ran while one was open for 0% of the time, Pallas kernels for 1%

profile of v3, /device:TPU:0, one launch (start us, length us, event | category | flops | bytes accessed | tf_op | source)
XLA Modules:
  0.0 29.9 jit_solution(677877513055326610)
XLA Ops:
  0.0 0.0 copy-start.2
  0.0 0.0 copy-start.3
  0.0 5.1 %collective-permute-start.1 = (bf16[16,512]{1,0:T(8,128)(2,1)}, bf16[16,512]{1,0:T(8,128)(2,1)S(1)}, u32[]{:S(2)}, u32[]{:S(2)}) collective-permute-start(bf16[16,512]{1,0:T(8,128)(2,1)} %refs_0_.1), channel_id=1, source_target_pairs={{0,3},{1,2},{3,0},{2,1},{4,7},{5,6},{7,4},{6,5},{8,11},{9,10},{11,... | collective-permute-start | bytes 49160 | tf_op jit(solution)/shard_map/ppermute | solution.py:130
  5.2 0.0 collective-permute-start
  5.2 2.9 %collective-permute-start.2 = (bf16[16,512]{1,0:T(8,128)(2,1)}, bf16[16,512]{1,0:T(8,128)(2,1)S(1)}, u32[]{:S(2)}, u32[]{:S(2)}) collective-permute-start(bf16[16,512]{1,0:T(8,128)(2,1)} %refs_0_.1), channel_id=1, source_target_pairs={{0,2},{1,0},{3,1},{2,3},{4,6},{5,4},{7,5},{6,7},{8,10},{9,8},{11,9... | collective-permute-start | bytes 49160 | tf_op jit(solution)/shard_map/ppermute | solution.py:130
  8.1 0.0 copy-start.1
  8.1 0.0 copy-done.3
  8.1 0.1 shard_map.47.pick
  8.3 0.0 collective-permute-done.1.refs_2_
  8.3 1.9 %collective-permute-done.refs_1_ = bf16[16,512]{1,0:T(8,128)(2,1)S(1)} collective-permute-done((bf16[16,512]{1,0:T(8,128)(2,1)}, bf16[16,512]{1,0:T(8,128)(2,1)S(1)}, u32[]{:S(2)}, u32[]{:S(2)}) %collective-permute-start) | collective-permute-done | bytes 16416 | tf_op jit(solution)/shard_map/ppermute | solution.py:130
  10.2 0.0 collective-permute-done.2.refs_3_
  10.2 0.0 copy-done.2
  10.2 0.0 copy-done
  10.2 0.9 %shard_map.48 = (f32[32,4096]{1,0:T(8,128)S(1)}, bf16[8,4096]{1,0:T(8,128)(2,1)S(1)}, bf16[24,4096]{1,0:T(8,128)(2,1)S(1)}) custom-call(bf16[64,64]{1,0:T(8,128)(2,1)S(1)} %shard_map.47.pick, bf16[16,512]{1,0:T(8,128)(2,1)S(1)} %copy-done.2, bf16[16,512]{1,0:T(8,128)(2,1)S(1)} %collective-permute-done.refs_1_, ...), custom_call_target="tpu_custom_call" | custom-call | flops 268435456 | bytes 4194304 | tf_op jit(solution)/shard_map/pallas_call | solution.py:18
  11.1 0.1 collective-permute-start.3
  11.2 0.5 %collective-permute-start.4 = (bf16[8,4096]{1,0:T(8,128)(2,1)S(1)}, bf16[8,4096]{1,0:T(8,128)(2,1)S(1)}, u32[]{:S(2)}, u32[]{:S(2)}) collective-permute-start(bf16[8,4096]{1,0:T(8,128)(2,1)S(1)} %get-tuple-element.22), channel_id=1, source_target_pairs={{0,4},{4,0},{8,12},{12,8},{16,20},{20,16},{24,28},{28,24},{1,5},{5... | collective-permute-start | bytes 196616 | tf_op jit(solution)/shard_map/ppermute | solution.py:127
  11.7 1.0 %collective-permute-done.4.got = bf16[8,4096]{1,0:T(8,128)(2,1)S(1)} collective-permute-done((bf16[8,4096]{1,0:T(8,128)(2,1)S(1)}, bf16[8,4096]{1,0:T(8,128)(2,1)S(1)}, u32[]{:S(2)}, u32[]{:S(2)}) %collective-permute-start.4) | collective-permute-done | bytes 65568 | tf_op jit(solution)/shard_map/ppermute | solution.py:127
  12.8 2.3 %collective-permute-start.5 = (bf16[8,4096]{1,0:T(8,128)(2,1)S(1)}, bf16[8,4096]{1,0:T(8,128)(2,1)S(1)}, u32[]{:S(2)}, u32[]{:S(2)}) collective-permute-start(bf16[8,4096]{1,0:T(8,128)(2,1)S(1)} %shard_map.50), channel_id=1, source_target_pairs={{0,24},{4,28},{8,16},{12,20},{16,8},{20,12},{24,0},{28,4},{1,25},{... | collective-permute-start | bytes 196616 | tf_op jit(solution)/shard_map/ppermute | solution.py:127
  15.1 0.0 collective-permute-done.3.got
  15.1 0.6 %collective-permute-start.6 = (bf16[8,4096]{1,0:T(8,128)(2,1)S(1)}, bf16[8,4096]{1,0:T(8,128)(2,1)S(1)}, u32[]{:S(2)}, u32[]{:S(2)}) collective-permute-start(bf16[8,4096]{1,0:T(8,128)(2,1)S(1)} %get-tuple-element.23), channel_id=1, source_target_pairs={{0,8},{4,12},{8,0},{12,4},{16,24},{20,28},{24,16},{28,20},{1,9},{5... | collective-permute-start | bytes 196616 | tf_op jit(solution)/shard_map/ppermute | solution.py:127
  15.7 0.7 %collective-permute-start.7 = (bf16[8,4096]{1,0:T(8,128)(2,1)S(1)}, bf16[8,4096]{1,0:T(8,128)(2,1)S(1)}, u32[]{:S(2)}, u32[]{:S(2)}) collective-permute-start(bf16[8,4096]{1,0:T(8,128)(2,1)S(1)} %get-tuple-element.24), channel_id=1, source_target_pairs={{0,16},{4,20},{8,24},{12,28},{16,0},{20,4},{24,8},{28,12},{1,17},{... | collective-permute-start | bytes 196616 | tf_op jit(solution)/shard_map/ppermute | solution.py:127
  16.4 1.9 %collective-permute-done.5.refs_0_ = bf16[8,4096]{1,0:T(8,128)(2,1)S(1)} collective-permute-done((bf16[8,4096]{1,0:T(8,128)(2,1)S(1)}, bf16[8,4096]{1,0:T(8,128)(2,1)S(1)}, u32[]{:S(2)}, u32[]{:S(2)}) %collective-permute-start.5) | collective-permute-done | bytes 65568 | tf_op jit(solution)/shard_map/ppermute | solution.py:127
  18.3 1.2 %collective-permute-done.6.refs_1_ = bf16[8,4096]{1,0:T(8,128)(2,1)S(1)} collective-permute-done((bf16[8,4096]{1,0:T(8,128)(2,1)S(1)}, bf16[8,4096]{1,0:T(8,128)(2,1)S(1)}, u32[]{:S(2)}, u32[]{:S(2)}) %collective-permute-start.6) | collective-permute-done | bytes 65568 | tf_op jit(solution)/shard_map/ppermute | solution.py:127
  19.5 0.5 %collective-permute-done.7.refs_2_ = bf16[8,4096]{1,0:T(8,128)(2,1)S(1)} collective-permute-done((bf16[8,4096]{1,0:T(8,128)(2,1)S(1)}, bf16[8,4096]{1,0:T(8,128)(2,1)S(1)}, u32[]{:S(2)}, u32[]{:S(2)}) %collective-permute-start.7) | collective-permute-done | bytes 65568 | tf_op jit(solution)/shard_map/ppermute | solution.py:127
  20.1 0.8 %collective-permute-start.8 = (bf16[2,4096]{1,0:T(2,128)(2,1)S(1)}, bf16[2,4096]{1,0:T(2,128)(2,1)S(1)}, u32[]{:S(2)}, u32[]{:S(2)}) collective-permute-start(bf16[2,4096]{1,0:T(2,128)(2,1)S(1)} %get-tuple-element.26), channel_id=1, source_target_pairs={{0,1},{1,0},{2,3},{3,2},{4,5},{5,4},{6,7},{7,6},{8,9},{9,8},{10,11... | collective-permute-start | bytes 49160 | tf_op jit(solution)/shard_map/ppermute | solution.py:174
  20.9 2.2 %collective-permute-start.9 = (bf16[2,4096]{1,0:T(2,128)(2,1)S(1)}, bf16[2,4096]{1,0:T(2,128)(2,1)S(1)}, u32[]{:S(2)}, u32[]{:S(2)}) collective-permute-start(bf16[2,4096]{1,0:T(2,128)(2,1)S(1)} %get-tuple-element.27), channel_id=1, source_target_pairs={{0,2},{1,3},{2,0},{3,1},{4,6},{5,7},{6,4},{7,5},{8,10},{9,11},{10,... | collective-permute-start | bytes 49160 | tf_op jit(solution)/shard_map/ppermute | solution.py:174
  23.1 1.4 %collective-permute-start.10 = (bf16[2,4096]{1,0:T(2,128)(2,1)S(1)}, bf16[2,4096]{1,0:T(2,128)(2,1)S(1)}, u32[]{:S(2)}, u32[]{:S(2)}) collective-permute-start(bf16[2,4096]{1,0:T(2,128)(2,1)S(1)} %get-tuple-element.28), channel_id=1, source_target_pairs={{0,3},{1,2},{2,1},{3,0},{4,7},{5,6},{6,5},{7,4},{8,11},{9,10},{10,... | collective-permute-start | bytes 49160 | tf_op jit(solution)/shard_map/ppermute | solution.py:174
  24.5 0.0 collective-permute-done.8.refs_1_
  24.5 1.0 %collective-permute-done.9.refs_2_ = bf16[2,4096]{1,0:T(2,128)(2,1)S(1)} collective-permute-done((bf16[2,4096]{1,0:T(2,128)(2,1)S(1)}, bf16[2,4096]{1,0:T(2,128)(2,1)S(1)}, u32[]{:S(2)}, u32[]{:S(2)}) %collective-permute-start.9) | collective-permute-done | bytes 16416 | tf_op jit(solution)/shard_map/ppermute | solution.py:174
  25.5 3.1 %collective-permute-done.10.refs_3_ = bf16[2,4096]{1,0:T(2,128)(2,1)S(1)} collective-permute-done((bf16[2,4096]{1,0:T(2,128)(2,1)S(1)}, bf16[2,4096]{1,0:T(2,128)(2,1)S(1)}, u32[]{:S(2)}, u32[]{:S(2)}) %collective-permute-start.10) | collective-permute-done | bytes 16416 | tf_op jit(solution)/shard_map/ppermute | solution.py:174
  28.7 0.0 copy-done.1
  28.7 1.3 %shard_map.52 = f32[2,8,512]{2,1,0:T(8,128)} custom-call(bf16[2,4096]{1,0:T(2,128)(2,1)S(1)} %get-tuple-element.25.refs_0_, bf16[2,4096]{1,0:T(2,128)(2,1)S(1)} %collective-permute-done.8.refs_1_, bf16[2,4096]{1,0:T(2,128)(2,1)S(1)} %collective-permute-done.9.refs_2_, bf16[2,4096]{1,0:T(2,128)(2,1)S(1)} %collective-permute-done.10.refs_3_, ...), custom_call_target="tpu_custom_call" | custom-call | flops 33554432 | bytes 4194304 | tf_op jit(solution)/shard_map/pallas_call | solution.py:18
  (5 shorter events, 0.1 us)
Async XLA Ops:
  0.0 10.2 %copy-start.2 = (bf16[16,512]{1,0:T(8,128)(2,1)S(1)}, bf16[16,512]{1,0:T(8,128)(2,1)}, u32[]{:S(2)}) copy-start(bf16[16,512]{1,0:T(8,128)(2,1)} %refs_0_.1) | copy-start | bytes 49156
  0.0 8.1 %copy-start.3 = (s32[64]{0:T(128)S(1)}, s32[64]{0:T(128)}, u32[]{:S(2)}) copy-start(s32[64]{0:T(128)} %param.6) | copy-start | bytes 772
  0.0 10.2 %copy-start = (bf16[512,4096]{1,0:T(8,128)(2,1)S(1)}, bf16[512,4096]{1,0:T(8,128)(2,1)}, u32[]{:S(2)}) copy-start(bf16[512,4096]{1,0:T(8,128)(2,1)} %refs_4_.2) | copy-start | bytes 12582916
  0.0 8.3 %collective-permute-start.1 = (bf16[16,512]{1,0:T(8,128)(2,1)}, bf16[16,512]{1,0:T(8,128)(2,1)S(1)}, u32[]{:S(2)}, u32[]{:S(2)}) collective-permute-start(bf16[16,512]{1,0:T(8,128)(2,1)} %refs_0_.1), channel_id=1, source_target_pairs={{0,3},{1,2},{3,0},{2,1},{4,7},{5,6},{7,4},{6,5},{8,11},{9,10},{11,... | collective-permute-start | bytes 49160 | tf_op jit(solution)/shard_map/ppermute | solution.py:130
  5.2 5.0 %collective-permute-start = (bf16[16,512]{1,0:T(8,128)(2,1)}, bf16[16,512]{1,0:T(8,128)(2,1)S(1)}, u32[]{:S(2)}, u32[]{:S(2)}) collective-permute-start(bf16[16,512]{1,0:T(8,128)(2,1)} %refs_0_.1), channel_id=1, source_target_pairs={{0,1},{1,3},{3,2},{2,0},{4,5},{5,7},{7,6},{6,4},{8,9},{9,11},{11,1... | collective-permute-start | bytes 49160 | tf_op jit(solution)/shard_map/ppermute | solution.py:130
  5.2 5.0 %collective-permute-start.2 = (bf16[16,512]{1,0:T(8,128)(2,1)}, bf16[16,512]{1,0:T(8,128)(2,1)S(1)}, u32[]{:S(2)}, u32[]{:S(2)}) collective-permute-start(bf16[16,512]{1,0:T(8,128)(2,1)} %refs_0_.1), channel_id=1, source_target_pairs={{0,2},{1,0},{3,1},{2,3},{4,6},{5,4},{7,5},{6,7},{8,10},{9,8},{11,9... | collective-permute-start | bytes 49160 | tf_op jit(solution)/shard_map/ppermute | solution.py:130
  8.1 20.5 %copy-start.1 = (bf16[2,2048,512]{2,1,0:T(8,128)(2,1)S(1)}, bf16[2,2048,512]{2,1,0:T(8,128)(2,1)}, u32[]{:S(2)}) copy-start(bf16[2,2048,512]{2,1,0:T(8,128)(2,1)} %refs_4_.3) | copy-start | bytes 12582916
  11.1 4.0 %collective-permute-start.3 = (bf16[24,4096]{1,0:T(8,128)(2,1)S(1)}, bf16[24,4096]{1,0:T(8,128)(2,1)S(1)}, u32[]{:S(2)}, u32[]{:S(2)}) collective-permute-start(bf16[24,4096]{1,0:T(8,128)(2,1)S(1)} %get-tuple-element.20), channel_id=1, source_target_pairs={{0,4},{4,0},{8,12},{12,8},{16,20},{20,16},{24,28},{28,24},{1,5},{5... | collective-permute-start | bytes 589832 | tf_op jit(solution)/shard_map/ppermute | solution.py:127
  11.2 1.5 %collective-permute-start.4 = (bf16[8,4096]{1,0:T(8,128)(2,1)S(1)}, bf16[8,4096]{1,0:T(8,128)(2,1)S(1)}, u32[]{:S(2)}, u32[]{:S(2)}) collective-permute-start(bf16[8,4096]{1,0:T(8,128)(2,1)S(1)} %get-tuple-element.22), channel_id=1, source_target_pairs={{0,4},{4,0},{8,12},{12,8},{16,20},{20,16},{24,28},{28,24},{1,5},{5... | collective-permute-start | bytes 196616 | tf_op jit(solution)/shard_map/ppermute | solution.py:127
  12.8 5.5 %collective-permute-start.5 = (bf16[8,4096]{1,0:T(8,128)(2,1)S(1)}, bf16[8,4096]{1,0:T(8,128)(2,1)S(1)}, u32[]{:S(2)}, u32[]{:S(2)}) collective-permute-start(bf16[8,4096]{1,0:T(8,128)(2,1)S(1)} %shard_map.50), channel_id=1, source_target_pairs={{0,24},{4,28},{8,16},{12,20},{16,8},{20,12},{24,0},{28,4},{1,25},{... | collective-permute-start | bytes 196616 | tf_op jit(solution)/shard_map/ppermute | solution.py:127
  15.1 4.3 %collective-permute-start.6 = (bf16[8,4096]{1,0:T(8,128)(2,1)S(1)}, bf16[8,4096]{1,0:T(8,128)(2,1)S(1)}, u32[]{:S(2)}, u32[]{:S(2)}) collective-permute-start(bf16[8,4096]{1,0:T(8,128)(2,1)S(1)} %get-tuple-element.23), channel_id=1, source_target_pairs={{0,8},{4,12},{8,0},{12,4},{16,24},{20,28},{24,16},{28,20},{1,9},{5... | collective-permute-start | bytes 196616 | tf_op jit(solution)/shard_map/ppermute | solution.py:127
  15.7 4.3 %collective-permute-start.7 = (bf16[8,4096]{1,0:T(8,128)(2,1)S(1)}, bf16[8,4096]{1,0:T(8,128)(2,1)S(1)}, u32[]{:S(2)}, u32[]{:S(2)}) collective-permute-start(bf16[8,4096]{1,0:T(8,128)(2,1)S(1)} %get-tuple-element.24), channel_id=1, source_target_pairs={{0,16},{4,20},{8,24},{12,28},{16,0},{20,4},{24,8},{28,12},{1,17},{... | collective-permute-start | bytes 196616 | tf_op jit(solution)/shard_map/ppermute | solution.py:127
  20.1 4.5 %collective-permute-start.8 = (bf16[2,4096]{1,0:T(2,128)(2,1)S(1)}, bf16[2,4096]{1,0:T(2,128)(2,1)S(1)}, u32[]{:S(2)}, u32[]{:S(2)}) collective-permute-start(bf16[2,4096]{1,0:T(2,128)(2,1)S(1)} %get-tuple-element.26), channel_id=1, source_target_pairs={{0,1},{1,0},{2,3},{3,2},{4,5},{5,4},{6,7},{7,6},{8,9},{9,8},{10,11... | collective-permute-start | bytes 49160 | tf_op jit(solution)/shard_map/ppermute | solution.py:174
  20.9 4.6 %collective-permute-start.9 = (bf16[2,4096]{1,0:T(2,128)(2,1)S(1)}, bf16[2,4096]{1,0:T(2,128)(2,1)S(1)}, u32[]{:S(2)}, u32[]{:S(2)}) collective-permute-start(bf16[2,4096]{1,0:T(2,128)(2,1)S(1)} %get-tuple-element.27), channel_id=1, source_target_pairs={{0,2},{1,3},{2,0},{3,1},{4,6},{5,7},{6,4},{7,5},{8,10},{9,11},{10,... | collective-permute-start | bytes 49160 | tf_op jit(solution)/shard_map/ppermute | solution.py:174
  23.1 5.5 %collective-permute-start.10 = (bf16[2,4096]{1,0:T(2,128)(2,1)S(1)}, bf16[2,4096]{1,0:T(2,128)(2,1)S(1)}, u32[]{:S(2)}, u32[]{:S(2)}) collective-permute-start(bf16[2,4096]{1,0:T(2,128)(2,1)S(1)} %get-tuple-element.28), channel_id=1, source_target_pairs={{0,3},{1,2},{2,1},{3,0},{4,7},{5,6},{6,5},{7,4},{8,11},{9,10},{10,... | collective-permute-start | bytes 49160 | tf_op jit(solution)/shard_map/ppermute | solution.py:174

commit v4 on v3

--- a/solution.py
+++ b/solution.py
@@ -38,7 +38,7 @@
 
 
 def turns_of(rows):
-    return [2 * n for n in sorted(range(1, rows // 2), key=lambda n: -n.bit_count())] + [0]
+    return [2 * n + 1 for n in sorted(range(1, rows // 2), key=lambda n: -n.bit_count())] + [0]
 
 
 def order_body(rows, cols, own, wanted, source):
@@ -50,8 +50,9 @@
     group, rest = lax.div(i, cols * each), lax.rem(i, cols * each)
     step, lane = lax.div(rest, each), lax.rem(rest, each)
     turns = turns_of(rows)
-    turn = lookup(turns + [t + 1 for t in turns], group)
-    slot = ((turn ^ r) * cols + (step ^ c)) * each + lane
+    turn = lookup(turns + [t ^ 1 for t in turns], group)
+    row = turn ^ r ^ jnp.where(step == 0, 0, 1)
+    slot = (row * cols + (step ^ c)) * each + lane
     wanted[...] = jnp.where(slot == p, 1.0, 0.0).astype(BF)
     ring = ring_of(cols)
     place = lookup([ring.index(n) for n in range(cols)], c + 0 * i)
@@ -171,7 +172,7 @@
         8 * block * width,
     )
     blocks = [outs[0]] + [
-        lax.ppermute(outs[k], "col", [(i, i ^ k) for i in range(cols)])
+        lax.ppermute(outs[k], ("row", "col"), [(i, i ^ (cols + k)) for i in range(rows * cols)])
         for k in range(1, cols)
     ]
     tiles = cols * width // keys.shape[1]

time: 30.1 us -> 28.8 us (0.957)
  starting transfers between devices: 16.7 us -> 16 us
  waiting for transfers between devices: 10.7 us -> 10.1 us
    ppermute x5, starting transfers between devices: 4.19 us -> 3.74 us  [along_row(): return lax.ppermute(x, 'row', [(i, i ^ k) for i in range(rows)])]
    ppermute x3, waiting for transfers between devices: 4.15 us -> 3.75 us  [shards(): lax.ppermute(outs[k], ('row', 'col'), [(i, i ^ cols + k) for i in range(r...]
where the time goes in v4:
time: 28.8 us; the launch traced here: 28.7 us
  starting transfers between devices  16 us (56%)
  waiting for transfers between devices  10.1 us (35%)
  Pallas kernels  2.48 us (9%)
    ppermute x3, starting transfers between devices, shards(): lax.ppermute(query, 'col', [(ring[i], ring[(i + k) % cols]) for i in rang...  8.07 us
    ppermute x5, waiting for transfers between devices, along_row(): return lax.ppermute(x, 'row', [(i, i ^ k) for i in range(rows)])  4.49 us
    ppermute x3, starting transfers between devices, shards(): lax.ppermute(outs[k], ('row', 'col'), [(i, i ^ cols + k) for i in range(r...  4.17 us
    ppermute x3, waiting for transfers between devices, shards(): lax.ppermute(outs[k], ('row', 'col'), [(i, i ^ cols + k) for i in range(r...  3.75 us
    ppermute x5, starting transfers between devices, along_row(): return lax.ppermute(x, 'row', [(i, i ^ k) for i in range(rows)])  3.74 us
    pallas_call x7, Pallas kernels, call(): pl.pallas_call(body, out_shape=outs, in_specs=[VMEM] * len(operands), out...  2.48 us
    ppermute x3, waiting for transfers between devices, shards(): lax.ppermute(query, 'col', [(ring[i], ring[(i + k) % cols]) for i in rang...  1.9 us
  transfers between devices with their start and end apart: 11, of which 7 were waited for; matrix products, arithmetic and copies ran while one was open for 0% of the time, Pallas kernels for 1%

profile of v4, /device:TPU:0, one launch (start us, length us, event | category | flops | bytes accessed | tf_op | source)
XLA Modules:
  0.0 28.7 jit_solution(17541795703525679112)
XLA Ops:
  0.0 0.0 copy-start.2
  0.0 0.0 copy-start.3
  0.0 5.1 %collective-permute-start.1 = (bf16[16,512]{1,0:T(8,128)(2,1)}, bf16[16,512]{1,0:T(8,128)(2,1)S(1)}, u32[]{:S(2)}, u32[]{:S(2)}) collective-permute-start(bf16[16,512]{1,0:T(8,128)(2,1)} %refs_0_.1), channel_id=1, source_target_pairs={{0,3},{1,2},{3,0},{2,1},{4,7},{5,6},{7,4},{6,5},{8,11},{9,10},{11,... | collective-permute-start | bytes 49160 | tf_op jit(solution)/shard_map/ppermute | solution.py:131
  5.2 0.0 collective-permute-start
  5.2 2.9 %collective-permute-start.2 = (bf16[16,512]{1,0:T(8,128)(2,1)}, bf16[16,512]{1,0:T(8,128)(2,1)S(1)}, u32[]{:S(2)}, u32[]{:S(2)}) collective-permute-start(bf16[16,512]{1,0:T(8,128)(2,1)} %refs_0_.1), channel_id=1, source_target_pairs={{0,2},{1,0},{3,1},{2,3},{4,6},{5,4},{7,5},{6,7},{8,10},{9,8},{11,9... | collective-permute-start | bytes 49160 | tf_op jit(solution)/shard_map/ppermute | solution.py:131
  8.1 0.0 copy-start.1
  8.1 0.0 copy-done.3
  8.1 0.1 shard_map.47.pick
  8.3 0.0 collective-permute-done.1.refs_2_
  8.3 1.9 %collective-permute-done.refs_1_ = bf16[16,512]{1,0:T(8,128)(2,1)S(1)} collective-permute-done((bf16[16,512]{1,0:T(8,128)(2,1)}, bf16[16,512]{1,0:T(8,128)(2,1)S(1)}, u32[]{:S(2)}, u32[]{:S(2)}) %collective-permute-start) | collective-permute-done | bytes 16416 | tf_op jit(solution)/shard_map/ppermute | solution.py:131
  10.2 0.0 collective-permute-done.2.refs_3_
  10.2 0.0 copy-done.2
  10.2 0.0 copy-done
  10.2 0.9 %shard_map.48 = (f32[32,4096]{1,0:T(8,128)S(1)}, bf16[8,4096]{1,0:T(8,128)(2,1)S(1)}, bf16[24,4096]{1,0:T(8,128)(2,1)S(1)}) custom-call(bf16[64,64]{1,0:T(8,128)(2,1)S(1)} %shard_map.47.pick, bf16[16,512]{1,0:T(8,128)(2,1)S(1)} %copy-done.2, bf16[16,512]{1,0:T(8,128)(2,1)S(1)} %collective-permute-done.refs_1_, ...), custom_call_target="tpu_custom_call" | custom-call | flops 268435456 | bytes 4194304 | tf_op jit(solution)/shard_map/pallas_call | solution.py:18
  11.1 0.1 collective-permute-start.3
  11.2 0.5 %collective-permute-start.4 = (bf16[8,4096]{1,0:T(8,128)(2,1)S(1)}, bf16[8,4096]{1,0:T(8,128)(2,1)S(1)}, u32[]{:S(2)}, u32[]{:S(2)}) collective-permute-start(bf16[8,4096]{1,0:T(8,128)(2,1)S(1)} %get-tuple-element.22), channel_id=1, source_target_pairs={{0,4},{4,0},{8,12},{12,8},{16,20},{20,16},{24,28},{28,24},{1,5},{5... | collective-permute-start | bytes 196616 | tf_op jit(solution)/shard_map/ppermute | solution.py:128
  11.7 1.0 %collective-permute-done.4.got = bf16[8,4096]{1,0:T(8,128)(2,1)S(1)} collective-permute-done((bf16[8,4096]{1,0:T(8,128)(2,1)S(1)}, bf16[8,4096]{1,0:T(8,128)(2,1)S(1)}, u32[]{:S(2)}, u32[]{:S(2)}) %collective-permute-start.4) | collective-permute-done | bytes 65568 | tf_op jit(solution)/shard_map/ppermute | solution.py:128
  12.8 2.2 %collective-permute-start.5 = (bf16[8,4096]{1,0:T(8,128)(2,1)S(1)}, bf16[8,4096]{1,0:T(8,128)(2,1)S(1)}, u32[]{:S(2)}, u32[]{:S(2)}) collective-permute-start(bf16[8,4096]{1,0:T(8,128)(2,1)S(1)} %shard_map.50), channel_id=1, source_target_pairs={{0,28},{4,24},{8,20},{12,16},{16,12},{20,8},{24,4},{28,0},{1,29},{... | collective-permute-start | bytes 196616 | tf_op jit(solution)/shard_map/ppermute | solution.py:128
  14.9 0.0 collective-permute-done.3.got
  15.0 0.5 %collective-permute-start.6 = (bf16[8,4096]{1,0:T(8,128)(2,1)S(1)}, bf16[8,4096]{1,0:T(8,128)(2,1)S(1)}, u32[]{:S(2)}, u32[]{:S(2)}) collective-permute-start(bf16[8,4096]{1,0:T(8,128)(2,1)S(1)} %get-tuple-element.23), channel_id=1, source_target_pairs={{0,12},{4,8},{8,4},{12,0},{16,28},{20,24},{24,20},{28,16},{1,13},{... | collective-permute-start | bytes 196616 | tf_op jit(solution)/shard_map/ppermute | solution.py:128
  15.5 0.5 %collective-permute-start.7 = (bf16[8,4096]{1,0:T(8,128)(2,1)S(1)}, bf16[8,4096]{1,0:T(8,128)(2,1)S(1)}, u32[]{:S(2)}, u32[]{:S(2)}) collective-permute-start(bf16[8,4096]{1,0:T(8,128)(2,1)S(1)} %get-tuple-element.24), channel_id=1, source_target_pairs={{0,20},{4,16},{8,28},{12,24},{16,4},{20,0},{24,12},{28,8},{1,21},{... | collective-permute-start | bytes 196616 | tf_op jit(solution)/shard_map/ppermute | solution.py:128
  16.0 1.7 %collective-permute-done.5.refs_0_ = bf16[8,4096]{1,0:T(8,128)(2,1)S(1)} collective-permute-done((bf16[8,4096]{1,0:T(8,128)(2,1)S(1)}, bf16[8,4096]{1,0:T(8,128)(2,1)S(1)}, u32[]{:S(2)}, u32[]{:S(2)}) %collective-permute-start.5) | collective-permute-done | bytes 65568 | tf_op jit(solution)/shard_map/ppermute | solution.py:128
  17.7 1.3 %collective-permute-done.6.refs_1_ = bf16[8,4096]{1,0:T(8,128)(2,1)S(1)} collective-permute-done((bf16[8,4096]{1,0:T(8,128)(2,1)S(1)}, bf16[8,4096]{1,0:T(8,128)(2,1)S(1)}, u32[]{:S(2)}, u32[]{:S(2)}) %collective-permute-start.6) | collective-permute-done | bytes 65568 | tf_op jit(solution)/shard_map/ppermute | solution.py:128
  19.0 0.5 %collective-permute-done.7.refs_2_ = bf16[8,4096]{1,0:T(8,128)(2,1)S(1)} collective-permute-done((bf16[8,4096]{1,0:T(8,128)(2,1)S(1)}, bf16[8,4096]{1,0:T(8,128)(2,1)S(1)}, u32[]{:S(2)}, u32[]{:S(2)}) %collective-permute-start.7) | collective-permute-done | bytes 65568 | tf_op jit(solution)/shard_map/ppermute | solution.py:128
  19.5 0.7 %collective-permute-start.8 = (bf16[2,4096]{1,0:T(2,128)(2,1)S(1)}, bf16[2,4096]{1,0:T(2,128)(2,1)S(1)}, u32[]{:S(2)}, u32[]{:S(2)}) collective-permute-start(bf16[2,4096]{1,0:T(2,128)(2,1)S(1)} %get-tuple-element.26), channel_id=1, source_target_pairs={{0,5},{1,4},{2,7},{3,6},{4,1},{5,0},{6,3},{7,2},{8,13},{9,12},{10,... | collective-permute-start | bytes 49160 | tf_op jit(solution)/shard_map/ppermute | solution.py:175
  20.2 2.2 %collective-permute-start.9 = (bf16[2,4096]{1,0:T(2,128)(2,1)S(1)}, bf16[2,4096]{1,0:T(2,128)(2,1)S(1)}, u32[]{:S(2)}, u32[]{:S(2)}) collective-permute-start(bf16[2,4096]{1,0:T(2,128)(2,1)S(1)} %get-tuple-element.27), channel_id=1, source_target_pairs={{0,6},{1,7},{2,4},{3,5},{4,2},{5,3},{6,0},{7,1},{8,14},{9,15},{10,... | collective-permute-start | bytes 49160 | tf_op jit(solution)/shard_map/ppermute | solution.py:175
  22.4 1.3 %collective-permute-start.10 = (bf16[2,4096]{1,0:T(2,128)(2,1)S(1)}, bf16[2,4096]{1,0:T(2,128)(2,1)S(1)}, u32[]{:S(2)}, u32[]{:S(2)}) collective-permute-start(bf16[2,4096]{1,0:T(2,128)(2,1)S(1)} %get-tuple-element.28), channel_id=1, source_target_pairs={{0,7},{1,6},{2,5},{3,4},{4,3},{5,2},{6,1},{7,0},{8,15},{9,14},{10,... | collective-permute-start | bytes 49160 | tf_op jit(solution)/shard_map/ppermute | solution.py:175
  23.7 0.0 collective-permute-done.8.refs_1_
  23.7 0.6 %collective-permute-done.9.refs_2_ = bf16[2,4096]{1,0:T(2,128)(2,1)S(1)} collective-permute-done((bf16[2,4096]{1,0:T(2,128)(2,1)S(1)}, bf16[2,4096]{1,0:T(2,128)(2,1)S(1)}, u32[]{:S(2)}, u32[]{:S(2)}) %collective-permute-start.9) | collective-permute-done | bytes 16416 | tf_op jit(solution)/shard_map/ppermute | solution.py:175
  24.2 3.2 %collective-permute-done.10.refs_3_ = bf16[2,4096]{1,0:T(2,128)(2,1)S(1)} collective-permute-done((bf16[2,4096]{1,0:T(2,128)(2,1)S(1)}, bf16[2,4096]{1,0:T(2,128)(2,1)S(1)}, u32[]{:S(2)}, u32[]{:S(2)}) %collective-permute-start.10) | collective-permute-done | bytes 16416 | tf_op jit(solution)/shard_map/ppermute | solution.py:175
  27.4 0.0 copy-done.1
  27.4 1.3 %shard_map.52 = f32[2,8,512]{2,1,0:T(8,128)} custom-call(bf16[2,4096]{1,0:T(2,128)(2,1)S(1)} %get-tuple-element.25.refs_0_, bf16[2,4096]{1,0:T(2,128)(2,1)S(1)} %collective-permute-done.8.refs_1_, bf16[2,4096]{1,0:T(2,128)(2,1)S(1)} %collective-permute-done.9.refs_2_, bf16[2,4096]{1,0:T(2,128)(2,1)S(1)} %collective-permute-done.10.refs_3_, ...), custom_call_target="tpu_custom_call" | custom-call | flops 33554432 | bytes 4194304 | tf_op jit(solution)/shard_map/pallas_call | solution.py:18
  (5 shorter events, 0.1 us)
Async XLA Ops:
  0.0 10.2 %copy-start.2 = (bf16[16,512]{1,0:T(8,128)(2,1)S(1)}, bf16[16,512]{1,0:T(8,128)(2,1)}, u32[]{:S(2)}) copy-start(bf16[16,512]{1,0:T(8,128)(2,1)} %refs_0_.1) | copy-start | bytes 49156
  0.0 8.1 %copy-start.3 = (s32[64]{0:T(128)S(1)}, s32[64]{0:T(128)}, u32[]{:S(2)}) copy-start(s32[64]{0:T(128)} %param.6) | copy-start | bytes 772
  0.0 10.2 %copy-start = (bf16[512,4096]{1,0:T(8,128)(2,1)S(1)}, bf16[512,4096]{1,0:T(8,128)(2,1)}, u32[]{:S(2)}) copy-start(bf16[512,4096]{1,0:T(8,128)(2,1)} %refs_4_.2) | copy-start | bytes 12582916
  0.0 8.3 %collective-permute-start.1 = (bf16[16,512]{1,0:T(8,128)(2,1)}, bf16[16,512]{1,0:T(8,128)(2,1)S(1)}, u32[]{:S(2)}, u32[]{:S(2)}) collective-permute-start(bf16[16,512]{1,0:T(8,128)(2,1)} %refs_0_.1), channel_id=1, source_target_pairs={{0,3},{1,2},{3,0},{2,1},{4,7},{5,6},{7,4},{6,5},{8,11},{9,10},{11,... | collective-permute-start | bytes 49160 | tf_op jit(solution)/shard_map/ppermute | solution.py:131
  5.2 5.0 %collective-permute-start = (bf16[16,512]{1,0:T(8,128)(2,1)}, bf16[16,512]{1,0:T(8,128)(2,1)S(1)}, u32[]{:S(2)}, u32[]{:S(2)}) collective-permute-start(bf16[16,512]{1,0:T(8,128)(2,1)} %refs_0_.1), channel_id=1, source_target_pairs={{0,1},{1,3},{3,2},{2,0},{4,5},{5,7},{7,6},{6,4},{8,9},{9,11},{11,1... | collective-permute-start | bytes 49160 | tf_op jit(solution)/shard_map/ppermute | solution.py:131
  5.2 5.0 %collective-permute-start.2 = (bf16[16,512]{1,0:T(8,128)(2,1)}, bf16[16,512]{1,0:T(8,128)(2,1)S(1)}, u32[]{:S(2)}, u32[]{:S(2)}) collective-permute-start(bf16[16,512]{1,0:T(8,128)(2,1)} %refs_0_.1), channel_id=1, source_target_pairs={{0,2},{1,0},{3,1},{2,3},{4,6},{5,4},{7,5},{6,7},{8,10},{9,8},{11,9... | collective-permute-start | bytes 49160 | tf_op jit(solution)/shard_map/ppermute | solution.py:131
  8.1 19.3 %copy-start.1 = (bf16[2,2048,512]{2,1,0:T(8,128)(2,1)S(1)}, bf16[2,2048,512]{2,1,0:T(8,128)(2,1)}, u32[]{:S(2)}) copy-start(bf16[2,2048,512]{2,1,0:T(8,128)(2,1)} %refs_4_.3) | copy-start | bytes 12582916
  11.1 3.8 %collective-permute-start.3 = (bf16[24,4096]{1,0:T(8,128)(2,1)S(1)}, bf16[24,4096]{1,0:T(8,128)(2,1)S(1)}, u32[]{:S(2)}, u32[]{:S(2)}) collective-permute-start(bf16[24,4096]{1,0:T(8,128)(2,1)S(1)} %get-tuple-element.20), channel_id=1, source_target_pairs={{0,4},{4,0},{8,12},{12,8},{16,20},{20,16},{24,28},{28,24},{1,5},{5... | collective-permute-start | bytes 589832 | tf_op jit(solution)/shard_map/ppermute | solution.py:128
  11.2 1.5 %collective-permute-start.4 = (bf16[8,4096]{1,0:T(8,128)(2,1)S(1)}, bf16[8,4096]{1,0:T(8,128)(2,1)S(1)}, u32[]{:S(2)}, u32[]{:S(2)}) collective-permute-start(bf16[8,4096]{1,0:T(8,128)(2,1)S(1)} %get-tuple-element.22), channel_id=1, source_target_pairs={{0,4},{4,0},{8,12},{12,8},{16,20},{20,16},{24,28},{28,24},{1,5},{5... | collective-permute-start | bytes 196616 | tf_op jit(solution)/shard_map/ppermute | solution.py:128
  12.8 4.9 %collective-permute-start.5 = (bf16[8,4096]{1,0:T(8,128)(2,1)S(1)}, bf16[8,4096]{1,0:T(8,128)(2,1)S(1)}, u32[]{:S(2)}, u32[]{:S(2)}) collective-permute-start(bf16[8,4096]{1,0:T(8,128)(2,1)S(1)} %shard_map.50), channel_id=1, source_target_pairs={{0,28},{4,24},{8,20},{12,16},{16,12},{20,8},{24,4},{28,0},{1,29},{... | collective-permute-start | bytes 196616 | tf_op jit(solution)/shard_map/ppermute | solution.py:128
  15.0 4.0 %collective-permute-start.6 = (bf16[8,4096]{1,0:T(8,128)(2,1)S(1)}, bf16[8,4096]{1,0:T(8,128)(2,1)S(1)}, u32[]{:S(2)}, u32[]{:S(2)}) collective-permute-start(bf16[8,4096]{1,0:T(8,128)(2,1)S(1)} %get-tuple-element.23), channel_id=1, source_target_pairs={{0,12},{4,8},{8,4},{12,0},{16,28},{20,24},{24,20},{28,16},{1,13},{... | collective-permute-start | bytes 196616 | tf_op jit(solution)/shard_map/ppermute | solution.py:128
  15.5 4.0 %collective-permute-start.7 = (bf16[8,4096]{1,0:T(8,128)(2,1)S(1)}, bf16[8,4096]{1,0:T(8,128)(2,1)S(1)}, u32[]{:S(2)}, u32[]{:S(2)}) collective-permute-start(bf16[8,4096]{1,0:T(8,128)(2,1)S(1)} %get-tuple-element.24), channel_id=1, source_target_pairs={{0,20},{4,16},{8,28},{12,24},{16,4},{20,0},{24,12},{28,8},{1,21},{... | collective-permute-start | bytes 196616 | tf_op jit(solution)/shard_map/ppermute | solution.py:128
  19.5 4.2 %collective-permute-start.8 = (bf16[2,4096]{1,0:T(2,128)(2,1)S(1)}, bf16[2,4096]{1,0:T(2,128)(2,1)S(1)}, u32[]{:S(2)}, u32[]{:S(2)}) collective-permute-start(bf16[2,4096]{1,0:T(2,128)(2,1)S(1)} %get-tuple-element.26), channel_id=1, source_target_pairs={{0,5},{1,4},{2,7},{3,6},{4,1},{5,0},{6,3},{7,2},{8,13},{9,12},{10,... | collective-permute-start | bytes 49160 | tf_op jit(solution)/shard_map/ppermute | solution.py:175
  20.2 4.1 %collective-permute-start.9 = (bf16[2,4096]{1,0:T(2,128)(2,1)S(1)}, bf16[2,4096]{1,0:T(2,128)(2,1)S(1)}, u32[]{:S(2)}, u32[]{:S(2)}) collective-permute-start(bf16[2,4096]{1,0:T(2,128)(2,1)S(1)} %get-tuple-element.27), channel_id=1, source_target_pairs={{0,6},{1,7},{2,4},{3,5},{4,2},{5,3},{6,0},{7,1},{8,14},{9,15},{10,... | collective-permute-start | bytes 49160 | tf_op jit(solution)/shard_map/ppermute | solution.py:175
  22.4 5.0 %collective-permute-start.10 = (bf16[2,4096]{1,0:T(2,128)(2,1)S(1)}, bf16[2,4096]{1,0:T(2,128)(2,1)S(1)}, u32[]{:S(2)}, u32[]{:S(2)}) collective-permute-start(bf16[2,4096]{1,0:T(2,128)(2,1)S(1)} %get-tuple-element.28), channel_id=1, source_target_pairs={{0,7},{1,6},{2,5},{3,4},{4,3},{5,2},{6,1},{7,0},{8,15},{9,14},{10,... | collective-permute-start | bytes 49160 | tf_op jit(solution)/shard_map/ppermute | solution.py:175

commit v5 on v4

--- a/solution.py
+++ b/solution.py
@@ -38,7 +38,7 @@
 
 
 def turns_of(rows):
-    return [2 * n + 1 for n in sorted(range(1, rows // 2), key=lambda n: -n.bit_count())] + [0]
+    return [2 * n + 1 for n in range(rows // 2 - 1, 0, -1)] + [0]
 
 
 def order_body(rows, cols, own, wanted, source):
@@ -50,7 +50,8 @@
     group, rest = lax.div(i, cols * each), lax.rem(i, cols * each)
     step, lane = lax.div(rest, each), lax.rem(rest, each)
     turns = turns_of(rows)
-    turn = lookup(turns + [t ^ 1 for t in turns], group)
+    away = [t ^ 1 for t in turns]
+    turn = lookup(turns[:1] + away[:1] + turns[1:] + away[1:], group)
     row = turn ^ r ^ jnp.where(step == 0, 0, 1)
     slot = (row * cols + (step ^ c)) * each + lane
     wanted[...] = jnp.where(slot == p, 1.0, 0.0).astype(BF)
@@ -67,25 +68,32 @@
     ).astype(BF)
 
 
-def product_body(pieces, pick, *refs):
-    queries, (database, keep, first, rest) = refs[:pieces], refs[pieces:]
+def lead_body(pieces, pick, *refs):
+    queries, (database, chosen, keep, away) = refs[:pieces], refs[pieces:]
     gathered = jnp.concatenate([q[...] for q in queries], axis=0)
-    chosen = jnp.dot(pick[...], gathered, preferred_element_type=F32).astype(BF)
-    half, block = keep.shape[0], first.shape[0]
-    value = jnp.dot(chosen, database[...], preferred_element_type=F32)
+    rows = jnp.dot(pick[...], gathered, preferred_element_type=F32).astype(BF)
+    block = keep.shape[0]
+    chosen[...] = rows[2 * block :]
+    value = jnp.dot(rows[: 2 * block], database[...], preferred_element_type=F32)
+    keep[...] = value[:block]
+    away[...] = value[block:].astype(BF)
+
+
+def bulk_body(chosen, database, keep, away):
+    value = jnp.dot(chosen[...], database[...], preferred_element_type=F32)
+    half = keep.shape[0]
     keep[...] = value[:half]
-    first[...] = value[half : half + block].astype(BF)
-    rest[...] = value[half + block :].astype(BF)
+    away[...] = value[half:].astype(BF)
 
 
 def first_body(keep, got, out):
-    out[...] = (keep[: out.shape[0]] + got[...].astype(F32)).astype(BF)
+    out[...] = (keep[...] + got[...].astype(F32)).astype(BF)
 
 
 def rest_body(keep, got, *outs):
     rows = outs[0].shape[0]
     for n, out in enumerate(outs):
-        value = keep[(n + 1) * rows : (n + 2) * rows] + got[n * rows : (n + 1) * rows].astype(F32)
+        value = keep[n * rows : (n + 1) * rows] + got[n * rows : (n + 1) * rows].astype(F32)
         out[...] = value.astype(out.dtype)
 
 
@@ -145,21 +153,29 @@
         2 * total**3,
         8 * total * total,
     )
-    keep, first, rest = call(
-        functools.partial(product_body, cols),
-        [S((half, width), F32), S((block, width), BF), S((half - block, width), BF)],
+    chosen, kept_first, first = call(
+        functools.partial(lead_body, cols),
+        [S((total - 2 * block, depth), BF), S((block, width), F32), S((block, width), BF)],
         [pick, query, *arrived, database],
-        2 * total * depth * width,
+        4 * block * depth * width,
         database.size * 2,
     )
     first = along_row(first, 1)
+    bulk = half - block
+    kept_rest, rest = call(
+        bulk_body,
+        [S((bulk, width), F32), S((bulk, width), BF)],
+        [chosen, database],
+        4 * bulk * depth * width,
+        database.size * 2,
+    )
     rest = along_row(rest, 1)
-    lead = call(first_body, S((block, width), BF), [keep, first], block * width, 8 * block * width)
+    lead = call(first_body, S((block, width), BF), [kept_first, first], block * width, 8 * block * width)
     lead = along_row(lead, turns[0])
     *others, kept = call(
         rest_body,
         [S((block, width), BF)] * (rows // 2 - 2) + [S((block, width), F32)],
-        [keep, rest],
+        [kept_rest, rest],
         half * width,
         6 * half * width,
     )

time: 28.8 us -> 29.4 us (1.021)
  Pallas kernels: 2.48 us -> 3.12 us
    pallas_call x7 -> x8, Pallas kernels: 2.48 us -> 3.12 us  [call(): pl.pallas_call(body, out_shape=outs, in_specs=[VMEM] * len(operands), out...]
where the time goes in v5:
time: 29.4 us; the launch traced here: 29.3 us
  starting transfers between devices  16 us (54%)
  waiting for transfers between devices  10.1 us (34%)
  Pallas kernels  3.12 us (11%)
    ppermute x3, starting transfers between devices, shards(): lax.ppermute(query, 'col', [(ring[i], ring[(i + k) % cols]) for i in rang...  8.07 us
    ppermute x5, waiting for transfers between devices, along_row(): return lax.ppermute(x, 'row', [(i, i ^ k) for i in range(rows)])  4.46 us
    ppermute x3, starting transfers between devices, shards(): lax.ppermute(outs[k], ('row', 'col'), [(i, i ^ cols + k) for i in range(r...  4.17 us
    ppermute x3, waiting for transfers between devices, shards(): lax.ppermute(outs[k], ('row', 'col'), [(i, i ^ cols + k) for i in range(r...  3.75 us
    ppermute x5, starting transfers between devices, along_row(): return lax.ppermute(x, 'row', [(i, i ^ k) for i in range(rows)])  3.73 us
    pallas_call x8, Pallas kernels, call(): pl.pallas_call(body, out_shape=outs, in_specs=[VMEM] * len(operands), out...  3.12 us
    ppermute x3, waiting for transfers between devices, shards(): lax.ppermute(query, 'col', [(ring[i], ring[(i + k) % cols]) for i in rang...  1.91 us
  transfers between devices with their start and end apart: 11, of which 7 were waited for; matrix products, arithmetic and copies ran while one was open for 0% of the time, Pallas kernels for 1%

profile of v5, /device:TPU:0, one launch (start us, length us, event | category | flops | bytes accessed | tf_op | source)
XLA Modules:
  0.0 29.3 jit_solution(1746695934740862618)
XLA Ops:
  0.0 0.0 copy-start.2
  0.0 0.0 copy-start.3
  0.0 5.1 %collective-permute-start.1 = (bf16[16,512]{1,0:T(8,128)(2,1)}, bf16[16,512]{1,0:T(8,128)(2,1)S(1)}, u32[]{:S(2)}, u32[]{:S(2)}) collective-permute-start(bf16[16,512]{1,0:T(8,128)(2,1)} %refs_0_.1), channel_id=1, source_target_pairs={{0,3},{1,2},{3,0},{2,1},{4,7},{5,6},{7,4},{6,5},{8,11},{9,10},{11,... | collective-permute-start | bytes 49160 | tf_op jit(solution)/shard_map/ppermute | solution.py:139
  5.2 0.0 collective-permute-start
  5.2 2.9 %collective-permute-start.2 = (bf16[16,512]{1,0:T(8,128)(2,1)}, bf16[16,512]{1,0:T(8,128)(2,1)S(1)}, u32[]{:S(2)}, u32[]{:S(2)}) collective-permute-start(bf16[16,512]{1,0:T(8,128)(2,1)} %refs_0_.1), channel_id=1, source_target_pairs={{0,2},{1,0},{3,1},{2,3},{4,6},{5,4},{7,5},{6,7},{8,10},{9,8},{11,9... | collective-permute-start | bytes 49160 | tf_op jit(solution)/shard_map/ppermute | solution.py:139
  8.1 0.0 copy-done.3
  8.1 0.1 shard_map.47.pick
  8.3 0.0 collective-permute-done.1.refs_2_
  8.3 1.9 %collective-permute-done.refs_1_ = bf16[16,512]{1,0:T(8,128)(2,1)S(1)} collective-permute-done((bf16[16,512]{1,0:T(8,128)(2,1)}, bf16[16,512]{1,0:T(8,128)(2,1)S(1)}, u32[]{:S(2)}, u32[]{:S(2)}) %collective-permute-start) | collective-permute-done | bytes 16416 | tf_op jit(solution)/shard_map/ppermute | solution.py:139
  10.2 0.0 collective-permute-done.2.refs_3_
  10.2 0.0 copy-done.2
  10.2 0.0 copy-done
  10.2 0.7 %shard_map.48 = (bf16[48,512]{1,0:T(8,128)(2,1)S(1)}, f32[8,4096]{1,0:T(8,128)S(1)}, bf16[8,4096]{1,0:T(8,128)(2,1)S(1)}) custom-call(bf16[64,64]{1,0:T(8,128)(2,1)S(1)} %shard_map.47.pick, bf16[16,512]{1,0:T(8,128)(2,1)S(1)} %copy-done.2, bf16[16,512]{1,0:T(8,128)(2,1)S(1)} %collective-permute-done.refs_1_, ...), custom_call_target="tpu_custom_call" | custom-call | flops 67108864 | bytes 4194304 | tf_op jit(solution)/shard_map/pallas_call | solution.py:18
  10.9 0.8 %shard_map.49 = (f32[24,4096]{1,0:T(8,128)S(1)}, bf16[24,4096]{1,0:T(8,128)(2,1)S(1)}) custom-call(bf16[48,512]{1,0:T(8,128)(2,1)S(1)} %get-tuple-element.21.chosen, bf16[512,4096]{1,0:T(8,128)(2,1)S(1)} %copy-done), custom_call_target="tpu_custom_call" | custom-call | flops 201326592 | bytes 4194304 | tf_op jit(solution)/shard_map/pallas_call | solution.py:18
  11.8 0.1 collective-permute-start.3
  11.8 0.5 %collective-permute-start.4 = (bf16[8,4096]{1,0:T(8,128)(2,1)S(1)}, bf16[8,4096]{1,0:T(8,128)(2,1)S(1)}, u32[]{:S(2)}, u32[]{:S(2)}) collective-permute-start(bf16[8,4096]{1,0:T(8,128)(2,1)S(1)} %get-tuple-element.26), channel_id=1, source_target_pairs={{0,4},{4,0},{8,12},{12,8},{16,20},{20,16},{24,28},{28,24},{1,5},{5... | collective-permute-start | bytes 196616 | tf_op jit(solution)/shard_map/ppermute | solution.py:136
  12.3 1.0 %collective-permute-done.4.got = bf16[8,4096]{1,0:T(8,128)(2,1)S(1)} collective-permute-done((bf16[8,4096]{1,0:T(8,128)(2,1)S(1)}, bf16[8,4096]{1,0:T(8,128)(2,1)S(1)}, u32[]{:S(2)}, u32[]{:S(2)}) %collective-permute-start.4) | collective-permute-done | bytes 65568 | tf_op jit(solution)/shard_map/ppermute | solution.py:136
  13.4 2.2 %collective-permute-start.5 = (bf16[8,4096]{1,0:T(8,128)(2,1)S(1)}, bf16[8,4096]{1,0:T(8,128)(2,1)S(1)}, u32[]{:S(2)}, u32[]{:S(2)}) collective-permute-start(bf16[8,4096]{1,0:T(8,128)(2,1)S(1)} %shard_map.51), channel_id=1, source_target_pairs={{0,28},{4,24},{8,20},{12,16},{16,12},{20,8},{24,4},{28,0},{1,29},{... | collective-permute-start | bytes 196616 | tf_op jit(solution)/shard_map/ppermute | solution.py:136
  15.5 0.0 collective-permute-done.3.got
  15.6 0.5 %collective-permute-start.6 = (bf16[8,4096]{1,0:T(8,128)(2,1)S(1)}, bf16[8,4096]{1,0:T(8,128)(2,1)S(1)}, u32[]{:S(2)}, u32[]{:S(2)}) collective-permute-start(bf16[8,4096]{1,0:T(8,128)(2,1)S(1)} %get-tuple-element.27), channel_id=1, source_target_pairs={{0,20},{4,16},{8,28},{12,24},{16,4},{20,0},{24,12},{28,8},{1,21},{... | collective-permute-start | bytes 196616 | tf_op jit(solution)/shard_map/ppermute | solution.py:136
  16.0 0.5 %collective-permute-start.7 = (bf16[8,4096]{1,0:T(8,128)(2,1)S(1)}, bf16[8,4096]{1,0:T(8,128)(2,1)S(1)}, u32[]{:S(2)}, u32[]{:S(2)}) collective-permute-start(bf16[8,4096]{1,0:T(8,128)(2,1)S(1)} %get-tuple-element.28), channel_id=1, source_target_pairs={{0,12},{4,8},{8,4},{12,0},{16,28},{20,24},{24,20},{28,16},{1,13},{... | collective-permute-start | bytes 196616 | tf_op jit(solution)/shard_map/ppermute | solution.py:136
  16.6 1.7 %collective-permute-done.5.refs_0_ = bf16[8,4096]{1,0:T(8,128)(2,1)S(1)} collective-permute-done((bf16[8,4096]{1,0:T(8,128)(2,1)S(1)}, bf16[8,4096]{1,0:T(8,128)(2,1)S(1)}, u32[]{:S(2)}, u32[]{:S(2)}) %collective-permute-start.5) | collective-permute-done | bytes 65568 | tf_op jit(solution)/shard_map/ppermute | solution.py:136
  18.3 1.4 %collective-permute-done.6.refs_1_ = bf16[8,4096]{1,0:T(8,128)(2,1)S(1)} collective-permute-done((bf16[8,4096]{1,0:T(8,128)(2,1)S(1)}, bf16[8,4096]{1,0:T(8,128)(2,1)S(1)}, u32[]{:S(2)}, u32[]{:S(2)}) %collective-permute-start.6) | collective-permute-done | bytes 65568 | tf_op jit(solution)/shard_map/ppermute | solution.py:136
  19.8 0.3 collective-permute-done.7.refs_2_
  20.1 0.7 %collective-permute-start.8 = (bf16[2,4096]{1,0:T(2,128)(2,1)S(1)}, bf16[2,4096]{1,0:T(2,128)(2,1)S(1)}, u32[]{:S(2)}, u32[]{:S(2)}) collective-permute-start(bf16[2,4096]{1,0:T(2,128)(2,1)S(1)} %get-tuple-element.30), channel_id=1, source_target_pairs={{0,5},{1,4},{2,7},{3,6},{4,1},{5,0},{6,3},{7,2},{8,13},{9,12},{10,... | collective-permute-start | bytes 49160 | tf_op jit(solution)/shard_map/ppermute | solution.py:191
  20.8 2.2 %collective-permute-start.9 = (bf16[2,4096]{1,0:T(2,128)(2,1)S(1)}, bf16[2,4096]{1,0:T(2,128)(2,1)S(1)}, u32[]{:S(2)}, u32[]{:S(2)}) collective-permute-start(bf16[2,4096]{1,0:T(2,128)(2,1)S(1)} %get-tuple-element.31), channel_id=1, source_target_pairs={{0,6},{1,7},{2,4},{3,5},{4,2},{5,3},{6,0},{7,1},{8,14},{9,15},{10,... | collective-permute-start | bytes 49160 | tf_op jit(solution)/shard_map/ppermute | solution.py:191
  23.0 1.3 %collective-permute-start.10 = (bf16[2,4096]{1,0:T(2,128)(2,1)S(1)}, bf16[2,4096]{1,0:T(2,128)(2,1)S(1)}, u32[]{:S(2)}, u32[]{:S(2)}) collective-permute-start(bf16[2,4096]{1,0:T(2,128)(2,1)S(1)} %get-tuple-element.32), channel_id=1, source_target_pairs={{0,7},{1,6},{2,5},{3,4},{4,3},{5,2},{6,1},{7,0},{8,15},{9,14},{10,... | collective-permute-start | bytes 49160 | tf_op jit(solution)/shard_map/ppermute | solution.py:191
  24.2 0.0 collective-permute-done.8.refs_1_
  24.2 0.6 %collective-permute-done.9.refs_2_ = bf16[2,4096]{1,0:T(2,128)(2,1)S(1)} collective-permute-done((bf16[2,4096]{1,0:T(2,128)(2,1)S(1)}, bf16[2,4096]{1,0:T(2,128)(2,1)S(1)}, u32[]{:S(2)}, u32[]{:S(2)}) %collective-permute-start.9) | collective-permute-done | bytes 16416 | tf_op jit(solution)/shard_map/ppermute | solution.py:191
  24.8 3.2 %collective-permute-done.10.refs_3_ = bf16[2,4096]{1,0:T(2,128)(2,1)S(1)} collective-permute-done((bf16[2,4096]{1,0:T(2,128)(2,1)S(1)}, bf16[2,4096]{1,0:T(2,128)(2,1)S(1)}, u32[]{:S(2)}, u32[]{:S(2)}) %collective-permute-start.10) | collective-permute-done | bytes 16416 | tf_op jit(solution)/shard_map/ppermute | solution.py:191
  28.0 0.0 copy-done.1
  28.0 1.3 %shard_map.53 = f32[2,8,512]{2,1,0:T(8,128)} custom-call(bf16[2,4096]{1,0:T(2,128)(2,1)S(1)} %get-tuple-element.29.refs_0_, bf16[2,4096]{1,0:T(2,128)(2,1)S(1)} %collective-permute-done.8.refs_1_, bf16[2,4096]{1,0:T(2,128)(2,1)S(1)} %collective-permute-done.9.refs_2_, bf16[2,4096]{1,0:T(2,128)(2,1)S(1)} %collective-permute-done.10.refs_3_, ...), custom_call_target="tpu_custom_call" | custom-call | flops 33554432 | bytes 4194304 | tf_op jit(solution)/shard_map/pallas_call | solution.py:18
  (6 shorter events, 0.1 us)
Async XLA Ops:
  0.0 10.2 %copy-start.2 = (bf16[16,512]{1,0:T(8,128)(2,1)S(1)}, bf16[16,512]{1,0:T(8,128)(2,1)}, u32[]{:S(2)}) copy-start(bf16[16,512]{1,0:T(8,128)(2,1)} %refs_0_.1) | copy-start | bytes 49156
  0.0 8.1 %copy-start.3 = (s32[64]{0:T(128)S(1)}, s32[64]{0:T(128)}, u32[]{:S(2)}) copy-start(s32[64]{0:T(128)} %param.6) | copy-start | bytes 772
  0.0 10.2 %copy-start = (bf16[512,4096]{1,0:T(8,128)(2,1)S(1)}, bf16[512,4096]{1,0:T(8,128)(2,1)}, u32[]{:S(2)}) copy-start(bf16[512,4096]{1,0:T(8,128)(2,1)} %database.1) | copy-start | bytes 12582916
  0.0 8.3 %collective-permute-start.1 = (bf16[16,512]{1,0:T(8,128)(2,1)}, bf16[16,512]{1,0:T(8,128)(2,1)S(1)}, u32[]{:S(2)}, u32[]{:S(2)}) collective-permute-start(bf16[16,512]{1,0:T(8,128)(2,1)} %refs_0_.1), channel_id=1, source_target_pairs={{0,3},{1,2},{3,0},{2,1},{4,7},{5,6},{7,4},{6,5},{8,11},{9,10},{11,... | collective-permute-start | bytes 49160 | tf_op jit(solution)/shard_map/ppermute | solution.py:139
  5.2 5.0 %collective-permute-start = (bf16[16,512]{1,0:T(8,128)(2,1)}, bf16[16,512]{1,0:T(8,128)(2,1)S(1)}, u32[]{:S(2)}, u32[]{:S(2)}) collective-permute-start(bf16[16,512]{1,0:T(8,128)(2,1)} %refs_0_.1), channel_id=1, source_target_pairs={{0,1},{1,3},{3,2},{2,0},{4,5},{5,7},{7,6},{6,4},{8,9},{9,11},{11,1... | collective-permute-start | bytes 49160 | tf_op jit(solution)/shard_map/ppermute | solution.py:139
  5.2 5.0 %collective-permute-start.2 = (bf16[16,512]{1,0:T(8,128)(2,1)}, bf16[16,512]{1,0:T(8,128)(2,1)S(1)}, u32[]{:S(2)}, u32[]{:S(2)}) collective-permute-start(bf16[16,512]{1,0:T(8,128)(2,1)} %refs_0_.1), channel_id=1, source_target_pairs={{0,2},{1,0},{3,1},{2,3},{4,6},{5,4},{7,5},{6,7},{8,10},{9,8},{11,9... | collective-permute-start | bytes 49160 | tf_op jit(solution)/shard_map/ppermute | solution.py:139
  8.3 19.7 %copy-start.1 = (bf16[2,2048,512]{2,1,0:T(8,128)(2,1)S(1)}, bf16[2,2048,512]{2,1,0:T(8,128)(2,1)}, u32[]{:S(2)}) copy-start(bf16[2,2048,512]{2,1,0:T(8,128)(2,1)} %refs_4_.3) | copy-start | bytes 12582916
  11.8 3.8 %collective-permute-start.3 = (bf16[24,4096]{1,0:T(8,128)(2,1)S(1)}, bf16[24,4096]{1,0:T(8,128)(2,1)S(1)}, u32[]{:S(2)}, u32[]{:S(2)}) collective-permute-start(bf16[24,4096]{1,0:T(8,128)(2,1)S(1)} %get-tuple-element.23), channel_id=1, source_target_pairs={{0,4},{4,0},{8,12},{12,8},{16,20},{20,16},{24,28},{28,24},{1,5},{5... | collective-permute-start | bytes 589832 | tf_op jit(solution)/shard_map/ppermute | solution.py:136
  11.8 1.5 %collective-permute-start.4 = (bf16[8,4096]{1,0:T(8,128)(2,1)S(1)}, bf16[8,4096]{1,0:T(8,128)(2,1)S(1)}, u32[]{:S(2)}, u32[]{:S(2)}) collective-permute-start(bf16[8,4096]{1,0:T(8,128)(2,1)S(1)} %get-tuple-element.26), channel_id=1, source_target_pairs={{0,4},{4,0},{8,12},{12,8},{16,20},{20,16},{24,28},{28,24},{1,5},{5... | collective-permute-start | bytes 196616 | tf_op jit(solution)/shard_map/ppermute | solution.py:136
  13.4 4.9 %collective-permute-start.5 = (bf16[8,4096]{1,0:T(8,128)(2,1)S(1)}, bf16[8,4096]{1,0:T(8,128)(2,1)S(1)}, u32[]{:S(2)}, u32[]{:S(2)}) collective-permute-start(bf16[8,4096]{1,0:T(8,128)(2,1)S(1)} %shard_map.51), channel_id=1, source_target_pairs={{0,28},{4,24},{8,20},{12,16},{16,12},{20,8},{24,4},{28,0},{1,29},{... | collective-permute-start | bytes 196616 | tf_op jit(solution)/shard_map/ppermute | solution.py:136
  15.6 4.2 %collective-permute-start.6 = (bf16[8,4096]{1,0:T(8,128)(2,1)S(1)}, bf16[8,4096]{1,0:T(8,128)(2,1)S(1)}, u32[]{:S(2)}, u32[]{:S(2)}) collective-permute-start(bf16[8,4096]{1,0:T(8,128)(2,1)S(1)} %get-tuple-element.27), channel_id=1, source_target_pairs={{0,20},{4,16},{8,28},{12,24},{16,4},{20,0},{24,12},{28,8},{1,21},{... | collective-permute-start | bytes 196616 | tf_op jit(solution)/shard_map/ppermute | solution.py:136
  16.0 4.0 %collective-permute-start.7 = (bf16[8,4096]{1,0:T(8,128)(2,1)S(1)}, bf16[8,4096]{1,0:T(8,128)(2,1)S(1)}, u32[]{:S(2)}, u32[]{:S(2)}) collective-permute-start(bf16[8,4096]{1,0:T(8,128)(2,1)S(1)} %get-tuple-element.28), channel_id=1, source_target_pairs={{0,12},{4,8},{8,4},{12,0},{16,28},{20,24},{24,20},{28,16},{1,13},{... | collective-permute-start | bytes 196616 | tf_op jit(solution)/shard_map/ppermute | solution.py:136
  20.1 4.2 %collective-permute-start.8 = (bf16[2,4096]{1,0:T(2,128)(2,1)S(1)}, bf16[2,4096]{1,0:T(2,128)(2,1)S(1)}, u32[]{:S(2)}, u32[]{:S(2)}) collective-permute-start(bf16[2,4096]{1,0:T(2,128)(2,1)S(1)} %get-tuple-element.30), channel_id=1, source_target_pairs={{0,5},{1,4},{2,7},{3,6},{4,1},{5,0},{6,3},{7,2},{8,13},{9,12},{10,... | collective-permute-start | bytes 49160 | tf_op jit(solution)/shard_map/ppermute | solution.py:191
  20.8 4.1 %collective-permute-start.9 = (bf16[2,4096]{1,0:T(2,128)(2,1)S(1)}, bf16[2,4096]{1,0:T(2,128)(2,1)S(1)}, u32[]{:S(2)}, u32[]{:S(2)}) collective-permute-start(bf16[2,4096]{1,0:T(2,128)(2,1)S(1)} %get-tuple-element.31), channel_id=1, source_target_pairs={{0,6},{1,7},{2,4},{3,5},{4,2},{5,3},{6,0},{7,1},{8,14},{9,15},{10,... | collective-permute-start | bytes 49160 | tf_op jit(solution)/shard_map/ppermute | solution.py:191
  23.0 5.0 %collective-permute-start.10 = (bf16[2,4096]{1,0:T(2,128)(2,1)S(1)}, bf16[2,4096]{1,0:T(2,128)(2,1)S(1)}, u32[]{:S(2)}, u32[]{:S(2)}) collective-permute-start(bf16[2,4096]{1,0:T(2,128)(2,1)S(1)} %get-tuple-element.32), channel_id=1, source_target_pairs={{0,7},{1,6},{2,5},{3,4},{4,3},{5,2},{6,1},{7,0},{8,15},{9,14},{10,... | collective-permute-start | bytes 49160 | tf_op jit(solution)/shard_map/ppermute | solution.py:191

commit v6 on v4

--- a/solution.py
+++ b/solution.py
@@ -38,7 +38,7 @@
 
 
 def turns_of(rows):
-    return [2 * n + 1 for n in sorted(range(1, rows // 2), key=lambda n: -n.bit_count())] + [0]
+    return [2 * n + 1 for n in range(rows // 2 - 1, 0, -1)] + [0]
 
 
 def order_body(rows, cols, own, wanted, source):
@@ -56,7 +56,9 @@
     wanted[...] = jnp.where(slot == p, 1.0, 0.0).astype(BF)
     ring = ring_of(cols)
     place = lookup([ring.index(n) for n in range(cols)], c + 0 * i)
-    origin = lookup(ring, lax.rem(place - lax.div(i, own) + cols, cols))
+    hop = lax.div(i, own)
+    hop = jnp.where(lax.rem(r + 0 * i, 2) == 0, hop, lax.rem(cols - hop, cols))
+    origin = lookup(ring, lax.rem(place - hop + cols, cols))
     source[...] = origin * own + lax.rem(i, own)
 
 
@@ -128,7 +130,15 @@
         return lax.ppermute(x, "row", [(i, i ^ k) for i in range(rows)])
 
     arrived = [
-        lax.ppermute(query, "col", [(ring[i], ring[(i + k) % cols]) for i in range(cols)])
+        lax.ppermute(
+            query,
+            ("row", "col"),
+            [
+                (r * cols + ring[i], r * cols + ring[(i + (cols - k if r % 2 else k)) % cols])
+                for r in range(rows)
+                for i in range(cols)
+            ],
+        )
         for k in range(1, cols)
     ]
     wanted, source = call(

time: 28.8 us -> 28.8 us (level)
  no operation moved by 1% of the time
where the time goes in v6:
time: 28.8 us; the launch traced here: 28.7 us
  starting transfers between devices  16 us (56%)
  waiting for transfers between devices  10.1 us (35%)
  Pallas kernels  2.49 us (9%)
    ppermute x3, starting transfers between devices, shards(): lax.ppermute(query, ('row', 'col'), [(r * cols + ring[i], r * cols + ring...  8.07 us
    ppermute x5, waiting for transfers between devices, along_row(): return lax.ppermute(x, 'row', [(i, i ^ k) for i in range(rows)])  4.46 us
    ppermute x3, starting transfers between devices, shards(): lax.ppermute(outs[k], ('row', 'col'), [(i, i ^ cols + k) for i in range(r...  4.17 us
    ppermute x3, waiting for transfers between devices, shards(): lax.ppermute(outs[k], ('row', 'col'), [(i, i ^ cols + k) for i in range(r...  3.75 us
    ppermute x5, starting transfers between devices, along_row(): return lax.ppermute(x, 'row', [(i, i ^ k) for i in range(rows)])  3.74 us
    pallas_call x7, Pallas kernels, call(): pl.pallas_call(body, out_shape=outs, in_specs=[VMEM] * len(operands), out...  2.49 us
    ppermute x3, waiting for transfers between devices, shards(): lax.ppermute(query, ('row', 'col'), [(r * cols + ring[i], r * cols + ring...  1.9 us
  transfers between devices with their start and end apart: 11, of which 7 were waited for; matrix products, arithmetic and copies ran while one was open for 0% of the time, Pallas kernels for 1%

profile of v6, /device:TPU:0, one launch (start us, length us, event | category | flops | bytes accessed | tf_op | source)
XLA Modules:
  0.0 28.7 jit_solution(11853530396944082322)
XLA Ops:
  0.0 0.0 copy-start.2
  0.0 0.0 copy-start.3
  0.0 5.1 %collective-permute-start.1 = (bf16[16,512]{1,0:T(8,128)(2,1)}, bf16[16,512]{1,0:T(8,128)(2,1)S(1)}, u32[]{:S(2)}, u32[]{:S(2)}) collective-permute-start(bf16[16,512]{1,0:T(8,128)(2,1)} %refs_0_.1), channel_id=1, source_target_pairs={{0,3},{1,2},{3,0},{2,1},{4,7},{5,6},{7,4},{6,5},{8,11},{9,10},{11,... | collective-permute-start | bytes 49160 | tf_op jit(solution)/shard_map/ppermute | solution.py:133
  5.2 0.0 collective-permute-start
  5.2 2.9 %collective-permute-start.2 = (bf16[16,512]{1,0:T(8,128)(2,1)}, bf16[16,512]{1,0:T(8,128)(2,1)S(1)}, u32[]{:S(2)}, u32[]{:S(2)}) collective-permute-start(bf16[16,512]{1,0:T(8,128)(2,1)} %refs_0_.1), channel_id=1, source_target_pairs={{0,2},{1,0},{3,1},{2,3},{4,5},{5,7},{7,6},{6,4},{8,10},{9,8},{11,9... | collective-permute-start | bytes 49160 | tf_op jit(solution)/shard_map/ppermute | solution.py:133
  8.1 0.0 copy-start.1
  8.1 0.0 copy-done.3
  8.2 0.1 shard_map.47.pick
  8.3 0.0 collective-permute-done.1.refs_2_
  8.3 1.9 %collective-permute-done.refs_1_ = bf16[16,512]{1,0:T(8,128)(2,1)S(1)} collective-permute-done((bf16[16,512]{1,0:T(8,128)(2,1)}, bf16[16,512]{1,0:T(8,128)(2,1)S(1)}, u32[]{:S(2)}, u32[]{:S(2)}) %collective-permute-start) | collective-permute-done | bytes 16416 | tf_op jit(solution)/shard_map/ppermute | solution.py:133
  10.2 0.0 collective-permute-done.2.refs_3_
  10.2 0.0 copy-done.2
  10.2 0.0 copy-done
  10.2 0.9 %shard_map.48 = (f32[32,4096]{1,0:T(8,128)S(1)}, bf16[8,4096]{1,0:T(8,128)(2,1)S(1)}, bf16[24,4096]{1,0:T(8,128)(2,1)S(1)}) custom-call(bf16[64,64]{1,0:T(8,128)(2,1)S(1)} %shard_map.47.pick, bf16[16,512]{1,0:T(8,128)(2,1)S(1)} %copy-done.2, bf16[16,512]{1,0:T(8,128)(2,1)S(1)} %collective-permute-done.refs_1_, ...), custom_call_target="tpu_custom_call" | custom-call | flops 268435456 | bytes 4194304 | tf_op jit(solution)/shard_map/pallas_call | solution.py:18
  11.1 0.1 collective-permute-start.3
  11.2 0.5 %collective-permute-start.4 = (bf16[8,4096]{1,0:T(8,128)(2,1)S(1)}, bf16[8,4096]{1,0:T(8,128)(2,1)S(1)}, u32[]{:S(2)}, u32[]{:S(2)}) collective-permute-start(bf16[8,4096]{1,0:T(8,128)(2,1)S(1)} %get-tuple-element.22), channel_id=1, source_target_pairs={{0,4},{4,0},{8,12},{12,8},{16,20},{20,16},{24,28},{28,24},{1,5},{5... | collective-permute-start | bytes 196616 | tf_op jit(solution)/shard_map/ppermute | solution.py:130
  11.7 1.0 %collective-permute-done.4.got = bf16[8,4096]{1,0:T(8,128)(2,1)S(1)} collective-permute-done((bf16[8,4096]{1,0:T(8,128)(2,1)S(1)}, bf16[8,4096]{1,0:T(8,128)(2,1)S(1)}, u32[]{:S(2)}, u32[]{:S(2)}) %collective-permute-start.4) | collective-permute-done | bytes 65568 | tf_op jit(solution)/shard_map/ppermute | solution.py:130
  12.8 2.2 %collective-permute-start.5 = (bf16[8,4096]{1,0:T(8,128)(2,1)S(1)}, bf16[8,4096]{1,0:T(8,128)(2,1)S(1)}, u32[]{:S(2)}, u32[]{:S(2)}) collective-permute-start(bf16[8,4096]{1,0:T(8,128)(2,1)S(1)} %shard_map.50), channel_id=1, source_target_pairs={{0,28},{4,24},{8,20},{12,16},{16,12},{20,8},{24,4},{28,0},{1,29},{... | collective-permute-start | bytes 196616 | tf_op jit(solution)/shard_map/ppermute | solution.py:130
  14.9 0.0 collective-permute-done.3.got
  15.0 0.5 %collective-permute-start.6 = (bf16[8,4096]{1,0:T(8,128)(2,1)S(1)}, bf16[8,4096]{1,0:T(8,128)(2,1)S(1)}, u32[]{:S(2)}, u32[]{:S(2)}) collective-permute-start(bf16[8,4096]{1,0:T(8,128)(2,1)S(1)} %get-tuple-element.23), channel_id=1, source_target_pairs={{0,20},{4,16},{8,28},{12,24},{16,4},{20,0},{24,12},{28,8},{1,21},{... | collective-permute-start | bytes 196616 | tf_op jit(solution)/shard_map/ppermute | solution.py:130
  15.4 0.5 %collective-permute-start.7 = (bf16[8,4096]{1,0:T(8,128)(2,1)S(1)}, bf16[8,4096]{1,0:T(8,128)(2,1)S(1)}, u32[]{:S(2)}, u32[]{:S(2)}) collective-permute-start(bf16[8,4096]{1,0:T(8,128)(2,1)S(1)} %get-tuple-element.24), channel_id=1, source_target_pairs={{0,12},{4,8},{8,4},{12,0},{16,28},{20,24},{24,20},{28,16},{1,13},{... | collective-permute-start | bytes 196616 | tf_op jit(solution)/shard_map/ppermute | solution.py:130
  16.0 1.7 %collective-permute-done.5.refs_0_ = bf16[8,4096]{1,0:T(8,128)(2,1)S(1)} collective-permute-done((bf16[8,4096]{1,0:T(8,128)(2,1)S(1)}, bf16[8,4096]{1,0:T(8,128)(2,1)S(1)}, u32[]{:S(2)}, u32[]{:S(2)}) %collective-permute-start.5) | collective-permute-done | bytes 65568 | tf_op jit(solution)/shard_map/ppermute | solution.py:130
  17.7 1.4 %collective-permute-done.6.refs_1_ = bf16[8,4096]{1,0:T(8,128)(2,1)S(1)} collective-permute-done((bf16[8,4096]{1,0:T(8,128)(2,1)S(1)}, bf16[8,4096]{1,0:T(8,128)(2,1)S(1)}, u32[]{:S(2)}, u32[]{:S(2)}) %collective-permute-start.6) | collective-permute-done | bytes 65568 | tf_op jit(solution)/shard_map/ppermute | solution.py:130
  19.1 0.3 collective-permute-done.7.refs_2_
  19.5 0.7 %collective-permute-start.8 = (bf16[2,4096]{1,0:T(2,128)(2,1)S(1)}, bf16[2,4096]{1,0:T(2,128)(2,1)S(1)}, u32[]{:S(2)}, u32[]{:S(2)}) collective-permute-start(bf16[2,4096]{1,0:T(2,128)(2,1)S(1)} %get-tuple-element.26), channel_id=1, source_target_pairs={{0,5},{1,4},{2,7},{3,6},{4,1},{5,0},{6,3},{7,2},{8,13},{9,12},{10,... | collective-permute-start | bytes 49160 | tf_op jit(solution)/shard_map/ppermute | solution.py:185
  20.1 2.2 %collective-permute-start.9 = (bf16[2,4096]{1,0:T(2,128)(2,1)S(1)}, bf16[2,4096]{1,0:T(2,128)(2,1)S(1)}, u32[]{:S(2)}, u32[]{:S(2)}) collective-permute-start(bf16[2,4096]{1,0:T(2,128)(2,1)S(1)} %get-tuple-element.27), channel_id=1, source_target_pairs={{0,6},{1,7},{2,4},{3,5},{4,2},{5,3},{6,0},{7,1},{8,14},{9,15},{10,... | collective-permute-start | bytes 49160 | tf_op jit(solution)/shard_map/ppermute | solution.py:185
  22.4 1.3 %collective-permute-start.10 = (bf16[2,4096]{1,0:T(2,128)(2,1)S(1)}, bf16[2,4096]{1,0:T(2,128)(2,1)S(1)}, u32[]{:S(2)}, u32[]{:S(2)}) collective-permute-start(bf16[2,4096]{1,0:T(2,128)(2,1)S(1)} %get-tuple-element.28), channel_id=1, source_target_pairs={{0,7},{1,6},{2,5},{3,4},{4,3},{5,2},{6,1},{7,0},{8,15},{9,14},{10,... | collective-permute-start | bytes 49160 | tf_op jit(solution)/shard_map/ppermute | solution.py:185
  23.6 0.0 collective-permute-done.8.refs_1_
  23.6 0.6 %collective-permute-done.9.refs_2_ = bf16[2,4096]{1,0:T(2,128)(2,1)S(1)} collective-permute-done((bf16[2,4096]{1,0:T(2,128)(2,1)S(1)}, bf16[2,4096]{1,0:T(2,128)(2,1)S(1)}, u32[]{:S(2)}, u32[]{:S(2)}) %collective-permute-start.9) | collective-permute-done | bytes 16416 | tf_op jit(solution)/shard_map/ppermute | solution.py:185
  24.2 3.2 %collective-permute-done.10.refs_3_ = bf16[2,4096]{1,0:T(2,128)(2,1)S(1)} collective-permute-done((bf16[2,4096]{1,0:T(2,128)(2,1)S(1)}, bf16[2,4096]{1,0:T(2,128)(2,1)S(1)}, u32[]{:S(2)}, u32[]{:S(2)}) %collective-permute-start.10) | collective-permute-done | bytes 16416 | tf_op jit(solution)/shard_map/ppermute | solution.py:185
  27.4 0.0 copy-done.1
  27.4 1.3 %shard_map.52 = f32[2,8,512]{2,1,0:T(8,128)} custom-call(bf16[2,4096]{1,0:T(2,128)(2,1)S(1)} %get-tuple-element.25.refs_0_, bf16[2,4096]{1,0:T(2,128)(2,1)S(1)} %collective-permute-done.8.refs_1_, bf16[2,4096]{1,0:T(2,128)(2,1)S(1)} %collective-permute-done.9.refs_2_, bf16[2,4096]{1,0:T(2,128)(2,1)S(1)} %collective-permute-done.10.refs_3_, ...), custom_call_target="tpu_custom_call" | custom-call | flops 33554432 | bytes 4194304 | tf_op jit(solution)/shard_map/pallas_call | solution.py:18
  (5 shorter events, 0.1 us)
Async XLA Ops:
  0.0 10.2 %copy-start.2 = (bf16[16,512]{1,0:T(8,128)(2,1)S(1)}, bf16[16,512]{1,0:T(8,128)(2,1)}, u32[]{:S(2)}) copy-start(bf16[16,512]{1,0:T(8,128)(2,1)} %refs_0_.1) | copy-start | bytes 49156
  0.0 8.1 %copy-start.3 = (s32[64]{0:T(128)S(1)}, s32[64]{0:T(128)}, u32[]{:S(2)}) copy-start(s32[64]{0:T(128)} %param.6) | copy-start | bytes 772
  0.0 10.2 %copy-start = (bf16[512,4096]{1,0:T(8,128)(2,1)S(1)}, bf16[512,4096]{1,0:T(8,128)(2,1)}, u32[]{:S(2)}) copy-start(bf16[512,4096]{1,0:T(8,128)(2,1)} %refs_4_.2) | copy-start | bytes 12582916
  0.0 8.3 %collective-permute-start.1 = (bf16[16,512]{1,0:T(8,128)(2,1)}, bf16[16,512]{1,0:T(8,128)(2,1)S(1)}, u32[]{:S(2)}, u32[]{:S(2)}) collective-permute-start(bf16[16,512]{1,0:T(8,128)(2,1)} %refs_0_.1), channel_id=1, source_target_pairs={{0,3},{1,2},{3,0},{2,1},{4,7},{5,6},{7,4},{6,5},{8,11},{9,10},{11,... | collective-permute-start | bytes 49160 | tf_op jit(solution)/shard_map/ppermute | solution.py:133
  5.2 5.0 %collective-permute-start = (bf16[16,512]{1,0:T(8,128)(2,1)}, bf16[16,512]{1,0:T(8,128)(2,1)S(1)}, u32[]{:S(2)}, u32[]{:S(2)}) collective-permute-start(bf16[16,512]{1,0:T(8,128)(2,1)} %refs_0_.1), channel_id=1, source_target_pairs={{0,1},{1,3},{3,2},{2,0},{4,6},{5,4},{7,5},{6,7},{8,9},{9,11},{11,1... | collective-permute-start | bytes 49160 | tf_op jit(solution)/shard_map/ppermute | solution.py:133
  5.2 5.0 %collective-permute-start.2 = (bf16[16,512]{1,0:T(8,128)(2,1)}, bf16[16,512]{1,0:T(8,128)(2,1)S(1)}, u32[]{:S(2)}, u32[]{:S(2)}) collective-permute-start(bf16[16,512]{1,0:T(8,128)(2,1)} %refs_0_.1), channel_id=1, source_target_pairs={{0,2},{1,0},{3,1},{2,3},{4,5},{5,7},{7,6},{6,4},{8,10},{9,8},{11,9... | collective-permute-start | bytes 49160 | tf_op jit(solution)/shard_map/ppermute | solution.py:133
  8.1 19.3 %copy-start.1 = (bf16[2,2048,512]{2,1,0:T(8,128)(2,1)S(1)}, bf16[2,2048,512]{2,1,0:T(8,128)(2,1)}, u32[]{:S(2)}) copy-start(bf16[2,2048,512]{2,1,0:T(8,128)(2,1)} %refs_4_.3) | copy-start | bytes 12582916
  11.1 3.8 %collective-permute-start.3 = (bf16[24,4096]{1,0:T(8,128)(2,1)S(1)}, bf16[24,4096]{1,0:T(8,128)(2,1)S(1)}, u32[]{:S(2)}, u32[]{:S(2)}) collective-permute-start(bf16[24,4096]{1,0:T(8,128)(2,1)S(1)} %get-tuple-element.20), channel_id=1, source_target_pairs={{0,4},{4,0},{8,12},{12,8},{16,20},{20,16},{24,28},{28,24},{1,5},{5... | collective-permute-start | bytes 589832 | tf_op jit(solution)/shard_map/ppermute | solution.py:130
  11.2 1.5 %collective-permute-start.4 = (bf16[8,4096]{1,0:T(8,128)(2,1)S(1)}, bf16[8,4096]{1,0:T(8,128)(2,1)S(1)}, u32[]{:S(2)}, u32[]{:S(2)}) collective-permute-start(bf16[8,4096]{1,0:T(8,128)(2,1)S(1)} %get-tuple-element.22), channel_id=1, source_target_pairs={{0,4},{4,0},{8,12},{12,8},{16,20},{20,16},{24,28},{28,24},{1,5},{5... | collective-permute-start | bytes 196616 | tf_op jit(solution)/shard_map/ppermute | solution.py:130
  12.8 4.9 %collective-permute-start.5 = (bf16[8,4096]{1,0:T(8,128)(2,1)S(1)}, bf16[8,4096]{1,0:T(8,128)(2,1)S(1)}, u32[]{:S(2)}, u32[]{:S(2)}) collective-permute-start(bf16[8,4096]{1,0:T(8,128)(2,1)S(1)} %shard_map.50), channel_id=1, source_target_pairs={{0,28},{4,24},{8,20},{12,16},{16,12},{20,8},{24,4},{28,0},{1,29},{... | collective-permute-start | bytes 196616 | tf_op jit(solution)/shard_map/ppermute | solution.py:130
  15.0 4.2 %collective-permute-start.6 = (bf16[8,4096]{1,0:T(8,128)(2,1)S(1)}, bf16[8,4096]{1,0:T(8,128)(2,1)S(1)}, u32[]{:S(2)}, u32[]{:S(2)}) collective-permute-start(bf16[8,4096]{1,0:T(8,128)(2,1)S(1)} %get-tuple-element.23), channel_id=1, source_target_pairs={{0,20},{4,16},{8,28},{12,24},{16,4},{20,0},{24,12},{28,8},{1,21},{... | collective-permute-start | bytes 196616 | tf_op jit(solution)/shard_map/ppermute | solution.py:130
  15.4 4.0 %collective-permute-start.7 = (bf16[8,4096]{1,0:T(8,128)(2,1)S(1)}, bf16[8,4096]{1,0:T(8,128)(2,1)S(1)}, u32[]{:S(2)}, u32[]{:S(2)}) collective-permute-start(bf16[8,4096]{1,0:T(8,128)(2,1)S(1)} %get-tuple-element.24), channel_id=1, source_target_pairs={{0,12},{4,8},{8,4},{12,0},{16,28},{20,24},{24,20},{28,16},{1,13},{... | collective-permute-start | bytes 196616 | tf_op jit(solution)/shard_map/ppermute | solution.py:130
  19.5 4.2 %collective-permute-start.8 = (bf16[2,4096]{1,0:T(2,128)(2,1)S(1)}, bf16[2,4096]{1,0:T(2,128)(2,1)S(1)}, u32[]{:S(2)}, u32[]{:S(2)}) collective-permute-start(bf16[2,4096]{1,0:T(2,128)(2,1)S(1)} %get-tuple-element.26), channel_id=1, source_target_pairs={{0,5},{1,4},{2,7},{3,6},{4,1},{5,0},{6,3},{7,2},{8,13},{9,12},{10,... | collective-permute-start | bytes 49160 | tf_op jit(solution)/shard_map/ppermute | solution.py:185
  20.1 4.1 %collective-permute-start.9 = (bf16[2,4096]{1,0:T(2,128)(2,1)S(1)}, bf16[2,4096]{1,0:T(2,128)(2,1)S(1)}, u32[]{:S(2)}, u32[]{:S(2)}) collective-permute-start(bf16[2,4096]{1,0:T(2,128)(2,1)S(1)} %get-tuple-element.27), channel_id=1, source_target_pairs={{0,6},{1,7},{2,4},{3,5},{4,2},{5,3},{6,0},{7,1},{8,14},{9,15},{10,... | collective-permute-start | bytes 49160 | tf_op jit(solution)/shard_map/ppermute | solution.py:185
  22.4 5.0 %collective-permute-start.10 = (bf16[2,4096]{1,0:T(2,128)(2,1)S(1)}, bf16[2,4096]{1,0:T(2,128)(2,1)S(1)}, u32[]{:S(2)}, u32[]{:S(2)}) collective-permute-start(bf16[2,4096]{1,0:T(2,128)(2,1)S(1)} %get-tuple-element.28), channel_id=1, source_target_pairs={{0,7},{1,6},{2,5},{3,4},{4,3},{5,2},{6,1},{7,0},{8,15},{9,14},{10,... | collective-permute-start | bytes 49160 | tf_op jit(solution)/shard_map/ppermute | solution.py:185
